TPU v7x, 256 devices: a whole 4x4x8 slice. The times are simulated.
256 devices in a mesh: px: 8 (over z_hi, y), py: 32 (over x, z_lo, core).
Axes of the slice: x: 4, y: 4, z: 8 (z_hi: 2, z_lo: 4; z = z_hi * 4 + z_lo), core: 2. Of those that a mesh axis runs over, the one named last changes fastest.
Arguments:
- velocity: float32 [3, 128, 128, 128], P(None, 'px', 'py'), may hold values from -4 to 4
- cotangent: float32 [3, 128, 128, 128], P(None, 'px', 'py'), may hold values from -6 to 6
- weight_in: bfloat16 [32, 3, 3, 3, 3], replicated, may hold values from -0.625 to 0.625
- bias_in: float32 [32], replicated, may hold values from -3 to 3
- weight_out: bfloat16 [6, 32, 3, 3, 3], replicated, may hold values from -0.21875 to 0.21875
Outputs:
- adjoint: float32 [3, 128, 128, 128], P(None, 'px', 'py')
All inputs are finite; a program needn't handle non-finite values.
Results may differ from a plain program's by a relative error of at most 0.00041.
Values sent between devices are 32-bit elements; how exact they have to be, the bound alone decides.
No kernel may reach another device: no remote copies, remote signals or barrier semaphores. Data moves between devices by JAX's collectives and lax.ppermute only.
A program may use at most 64 MiB of HBM per device.

v0:
```python
import functools
import math

import jax
import jax.numpy as jnp
import ml_dtypes
import numpy as np
from jax import lax
from jax.experimental import pallas as pl
from jax.experimental.pallas import tpu as pltpu
from jax.sharding import PartitionSpec as P

N = 128
PX = 8
PY = 32
time_step = 0.005
spacing = 2.0 * math.pi / N
bf16 = jnp.bfloat16
f32 = jnp.float32
PRE = 80
STR = 144


def halves(table):
    table = np.asarray(table, np.float64)
    high = table.astype(np.float32).astype(ml_dtypes.bfloat16)
    low = (table - high.astype(np.float64)).astype(np.float32).astype(ml_dtypes.bfloat16)
    return np.stack([high, low])


def complex_form(table):
    return np.block([[table.real, table.imag], [-table.imag, table.real]])


@functools.cache
def constants():
    z = np.arange(N)
    kz = np.arange(N // 2)
    angle = 2 * np.pi * ((kz[:, None] * z[None]) % N) / N
    cos, sin = np.cos(angle), np.sin(angle)
    weight = np.where(kz == 0, 1.0, 2.0)[:, None] / float(N) ** 3

    def pair(first, second):
        return np.stack([first, second], 1).reshape(N, N)

    forward_z = np.stack([halves(pair(cos, -sin)), halves(pair(sin, cos))])
    backward_z = np.stack(
        [halves(pair(cos * weight, -sin * weight)), halves(pair(sin * weight, cos * weight))]
    )
    a, b = np.arange(PX), np.arange(PY)
    y4, x16 = np.arange(4), np.arange(16)
    phase = a[:, None, None, None] * a[None, None, :, None] / PX
    phase = phase + b[None, :, None, None] * b[None, None, None, :] / PY
    rows = np.exp(-2j * np.pi * phase.reshape(256, 256))
    row_forward = halves(np.concatenate([rows.real, rows.imag], 0))
    row_backward = halves(np.concatenate([rows.real, rows.imag], 1))
    phase = a[:, None, None, None] * x16 + b[None, :, None, None] * y4[:, None]
    twiddle = np.exp(-2j * np.pi * phase.reshape(256, 64) / N)
    twiddle = np.tile(twiddle, (1, 2))
    twiddle = np.stack([twiddle.real, twiddle.imag]).astype(np.float32)
    phase = y4[:, None, None, None] * y4[:, None] / 4 + x16[:, None, None] * x16 / 16
    lanes = np.exp(-2j * np.pi * phase.reshape(64, 64))
    lane_forward = halves(complex_form(np.kron(np.eye(2), lanes)))
    m, l = np.broadcast_arrays(
        a[:, None, None, None] + 8 * x16, b[None, :, None, None] + 32 * y4[:, None]
    )
    m, l = m.reshape(256, 64), l.reshape(256, 64)
    kx, ky = np.where(m > 64, m - N, m), np.where(l > 64, l - N, l)
    square = np.tile(kx * kx + ky * ky, (1, 2))
    retain = np.tile((m != 64) & (l != 64), (1, 2))
    waves = np.stack([np.concatenate([kx, ky], 1), square, retain]).astype(np.float32)
    r = np.arange(24)
    xe = np.where(r < 19, r, r - 24)
    lane_backward, twiddle_back = [], []
    for part in range(2):
        ye = np.arange(5) + (5 * part - 3)
        phase = y4[:, None, None, None] * ye[:, None] / 4 + x16[:, None, None] * xe / 16
        table = np.pad(np.exp(2j * np.pi * phase.reshape(64, 120)), ((0, 0), (0, 8)))
        for component in range(2):
            pick = np.eye(2)[:, component : component + 1]
            lane_backward.append(halves(complex_form(np.kron(pick, table))))
        phase = a[:, None, None, None] * xe + b[None, :, None, None] * ye[:, None]
        table = np.pad(np.exp(2j * np.pi * phase.reshape(256, 120) / N), ((0, 0), (0, 8)))
        twiddle_back.append(np.stack([table.real, table.imag]))
    lane_backward = np.stack(lane_backward).reshape(2, 2, 2, 256, 256)
    twiddle_back = np.stack(twiddle_back).astype(np.float32)
    select_in = np.zeros((3, 3, 3, 3, 3 * PRE))
    select_out = np.zeros((6, 3, 3, 3, 3 * STR))
    select_back = np.zeros((3, 6, 3, 16, 3, 3, 3, 3))
    for dx in range(3):
        for dz in range(3):
            for dy in range(3):
                for c in range(3):
                    select_in[c, dx, dy, dz, dx * PRE + dz * 24 + c * 8 + dy] = 1
                for s in range(6):
                    column = dx * STR + dz * 48 + s * 8 + dy
                    select_out[s, 2 - dx, 2 - dy, 2 - dz, column] = 1
            for c in range(3):
                for yo in range(4):
                    for yi in range(6):
                        if 0 <= yo + 2 - yi < 3:
                            select_back[dx, yi, dz, c * 4 + yo, c, 2 - dx, yo + 2 - yi, dz] = 1
    select_in = select_in.reshape(81, 3 * PRE).astype(ml_dtypes.bfloat16)
    select_out = select_out.reshape(162, 3 * STR).astype(ml_dtypes.bfloat16)
    select_back = select_back.reshape(18 * 48, 81).astype(ml_dtypes.bfloat16)
    return dict(
        forward_z=forward_z,
        backward_z=backward_z,
        row_forward=row_forward,
        row_backward=row_backward,
        twiddle=twiddle,
        lane_forward=lane_forward,
        waves=waves,
        lane_backward=lane_backward,
        twiddle_back=twiddle_back,
        select_in=select_in,
        select_out=select_out,
        select_back=select_back,
    )


def split(value):
    high = value.astype(bf16)
    return high, (value - high.astype(f32)).astype(bf16)


def product(left, right, over=(1, 0)):
    dims = (((over[0],), (over[1],)), ((), ()))

    def one(a, b):
        return lax.dot_general(a, b, dims, preferred_element_type=f32)

    return one(left[0], right[0]) + (one(left[1], right[0]) + one(left[0], right[1]))


def transform_z(source, table, out):
    blocks = [[source[pl.ds(c * 64 + y, 16, stride=4), :] for y in range(4)] for c in range(3)]
    first = jnp.concatenate(blocks[0] + blocks[1], 0)
    second = jnp.concatenate(blocks[2] + blocks[2], 0)
    for tile, cells in enumerate((first, second)):
        modes = product((table[tile, 0], table[tile, 1]), split(cells), (1, 1))
        for copy in range(2):
            out[pl.ds(2 * copy + tile, 128, stride=4), :] = modes


def project(
    which,
    source,
    row_forward,
    twiddle,
    lane_forward,
    waves,
    lane_backward,
    twiddle_back,
    row_backward,
    out,
):
    part = which[0]
    kz = which[1].astype(f32)
    tiles = [source[pl.ds(tile, 256, stride=2), :] for tile in range(2)]
    mixed = product((row_forward[0], row_forward[1]), split(jnp.concatenate(tiles, 1)))
    cos, sin = twiddle[0], twiddle[1]
    spectrum = []
    for tile in range(2):
        real = mixed[:256, tile * 128 : tile * 128 + 128]
        imag = mixed[256:, tile * 128 : tile * 128 + 128]
        turned = jnp.concatenate([real * cos - imag * sin, real * sin + imag * cos], 1)
        spectrum.append(product(split(turned), (lane_forward[0], lane_forward[1])))
    wave, square, retain = waves[0], waves[1], waves[2]
    inverse = 1.0 / jnp.maximum(square + kz * kz, 1.0)
    (hr, hi), (vr, vi) = [(s[:, :128], s[:, 128:]) for s in spectrum]
    flat_r, flat_i = hr * wave, hi * wave
    flat_r = flat_r + pltpu.roll(flat_r, 64, 1)
    flat_i = flat_i + pltpu.roll(flat_i, 64, 1)
    dot_r = (flat_r + kz * vi) * inverse
    dot_i = (flat_i - kz * vr) * inverse
    flat = jnp.concatenate([(hr - wave * dot_r) * retain, (hi - wave * dot_i) * retain], 1)
    upright = jnp.concatenate([(vr + kz * dot_i) * retain, (vi - kz * dot_r) * retain], 1)
    flat, upright = split(flat), split(upright)
    cos, sin = twiddle_back[part, 0], twiddle_back[part, 1]
    parts = []
    for component in range(3):
        matrix = lane_backward.at[part, component % 2]
        cells = product(upright if component == 2 else flat, (matrix[0], matrix[1]))
        real, imag = cells[:, :128], cells[:, 128:]
        parts.append(jnp.concatenate([real * cos - imag * sin, real * sin + imag * cos], 0))
    result = product((row_backward[0], row_backward[1]), split(jnp.concatenate(parts, 1)))
    for component in range(3):
        block = result[:, component * 128 : component * 128 + 128]
        out[pl.ds(component, 256, stride=3), :] = block


def extend_x(source, low, high, out):
    for c in range(3):
        for y in range(4):
            base = (c * 4 + y) * 24
            out[pl.ds(base + 16, 8), :] = jnp.zeros((8, 128), f32)
            out[pl.ds(base, 16), :] = source[pl.ds(c * 64 + y, 16, stride=4), :]
            out[pl.ds(base + 16, 3), :] = high[pl.ds(c * 12 + y, 3, stride=4), :]
            out[pl.ds(base + 21, 3), :] = low[pl.ds(c * 12 + y, 3, stride=4), :]


def sixth(at):
    near, middle, far = [at(k) - at(-k) for k in (1, 2, 3)]
    return (45.0 * near - 9.0 * middle + far) * (1.0 / (60.0 * spacing))


def rolled(block, axis):
    return lambda k: pltpu.roll(block, (-k) % block.shape[axis], axis)


def prepare(
    own,
    low,
    high,
    kernel_in,
    kernel_out,
    bias,
    select_in,
    select_out,
    select_back,
    field,
    slope,
    slants,
    banded_out,
    banded_back,
    banded_in,
    slabs,
):
    for c in range(3):
        field[pl.ds(c * 240, 72), :] = low[pl.ds(c * 72, 72), :]
        field[pl.ds(c * 240 + 72, 96), :] = own[pl.ds(c * 96, 96), :]
        field[pl.ds(c * 240 + 168, 72), :] = high[pl.ds(c * 72, 72), :]
    over_rows = (((0,), (0,)), ((), ()))
    band = lax.dot_general(kernel_in[...], select_in[...], over_rows, preferred_element_type=f32)
    for yo in range(6):
        moved = band if yo == 0 else jnp.concatenate([jnp.zeros((32, yo), f32), band[:, :-yo]], 1)
        banded_in[pl.ds(yo * 32, 32), :] = moved.astype(bf16)
    band = lax.dot_general(kernel_out[...], select_out[...], over_rows, preferred_element_type=f32)
    for yo in range(6):
        moved = band if yo == 0 else jnp.concatenate([jnp.zeros((32, yo), f32), band[:, :-yo]], 1)
        banded_out[pl.ds(yo * 32, 32), :] = moved.astype(bf16)
    band = jnp.dot(select_back[...], kernel_in[...], preferred_element_type=f32).astype(bf16)
    for block in range(18):
        banded_back[:, pl.ds(block * 32, 32)] = band[block * 48 : block * 48 + 48]

    def gather(i, carry):
        row = lax.rem(i + 22, 24)
        parts = [field[pl.ds(c * 240 + 24 + row, 8, stride=24), :] for c in range(3)]
        slab = jnp.concatenate(parts, 0)
        shifts = [pltpu.roll(slab, 1, 1), slab, pltpu.roll(slab, 127, 1)]
        slab = jnp.concatenate(shifts + [jnp.zeros((8, 128), f32)], 0)
        slabs[pl.ds(pl.multiple_of(i * PRE, 16), PRE), :] = slab.astype(bf16)
        return carry

    lax.fori_loop(0, 20, gather, 0)

    def activate(i, carry):
        cells = slabs[pl.ds(pl.multiple_of(i * PRE, 16), 3 * PRE), :]
        value = jnp.dot(banded_in[...], cells, preferred_element_type=f32) + bias[...]
        value = jnp.tanh(value)
        slope[pl.ds(pl.multiple_of(i * 192, 8), 192), :] = 1.0 - value * value
        return carry

    lax.fori_loop(0, 18, activate, 0)
    for a in range(3):
        for y in range(4):
            base = a * 240 + (y + 3) * 24
            block = field[pl.ds(base, 24), :]
            inner = block[:16]
            along = [
                sixth(rolled(block, 0))[:16],
                sixth(lambda k, base=base: field[pl.ds(base + 24 * k, 16), :]),
                sixth(rolled(inner, 1)),
            ]
            for c in range(3):
                slants[pl.ds(((a * 3 + c) * 4 + y) * 16, 16), :] = along[c]


def finish(
    modes,
    table,
    field,
    slope,
    slants,
    banded_out,
    banded_back,
    out,
    lam,
    stress,
    slabs,
    adjoint,
    closure,
):
    for c in range(3):
        matrix = table.at[c // 2]
        for part in range(2):
            cells = split(modes[pl.ds(part * 3 + c, 128, stride=6), :])
            values = product(cells, (matrix[0], matrix[1]), (0, 0))
            lam[pl.ds(c * 240 + part * 120, 120), :] = values[:120]
    scale = 1.0 / (2.0 * spacing)
    for y in range(8):
        blocks = [lam[pl.ds(c * 240 + (y + 1) * 24, 24), :] for c in range(3)]
        along_x = [(pltpu.roll(b, 23, 0) - pltpu.roll(b, 1, 0)) * scale for b in blocks]
        along_z = [(pltpu.roll(b, 127, 1) - pltpu.roll(b, 1, 1)) * scale for b in blocks]
        along_y = [
            (lam[pl.ds(c * 240 + (y + 2) * 24, 24), :] - lam[pl.ds(c * 240 + y * 24, 24), :]) * scale
            for c in range(3)
        ]
        values = [
            along_x[0],
            along_y[1],
            along_z[2],
            along_y[0] + along_x[1],
            along_z[0] + along_x[2],
            along_z[1] + along_y[2],
        ]
        for s in range(6):
            stress[pl.ds((s * 8 + y) * 24, 24), :] = values[s]

    def gather(i, carry):
        row = lax.rem(i + 22, 24)
        slab = stress[pl.ds(row, 48, stride=24), :]
        shifts = [pltpu.roll(slab, 1, 1), slab, pltpu.roll(slab, 127, 1)]
        slab = jnp.concatenate(shifts, 0)
        slabs[pl.ds(pl.multiple_of(i * STR, 16), STR), :] = slab.astype(bf16)
        return carry

    lax.fori_loop(0, 20, gather, 0)

    def hidden(i, carry):
        cells = slabs[pl.ds(pl.multiple_of(i * STR, 16), 3 * STR), :]
        value = jnp.dot(banded_out[...], cells, preferred_element_type=f32)
        rows = pl.ds(pl.multiple_of(i * 192, 16), 192)
        adjoint[rows, :] = (value * slope[rows, :]).astype(bf16)
        return carry

    lax.fori_loop(0, 18, hidden, 0)

    def back(i, carry):
        cells = adjoint[pl.ds(pl.multiple_of(i * 192, 16), 576), :]
        value = jnp.dot(banded_back[...], cells, preferred_element_type=f32)
        total = value[16:32] + pltpu.roll(value[:16], 127, 1) + pltpu.roll(value[32:], 1, 1)
        closure[pl.ds(pl.multiple_of(i * 16, 16), 16), :] = total
        return carry

    lax.fori_loop(0, 16, back, 0)
    for c in range(3):
        across = [
            lam[pl.ds(c * 240 + y * 24, 16), :] * field[pl.ds(240 + y * 24, 16), :]
            for y in range(10)
        ]
        for y in range(4):
            base = (y + 3) * 24
            block = lam[pl.ds(c * 240 + base, 24), :]
            total = sixth(rolled(block * field[pl.ds(base, 24), :], 0))[:16]
            total = total + sixth(lambda k, y=y: across[y + 3 + k])
            total = total + sixth(rolled(block[:16] * field[pl.ds(480 + base, 16), :], 1))
            crossed = [
                lam[pl.ds(a * 240 + base, 16), :] * slants[pl.ds(((a * 3 + c) * 4 + y) * 16, 16), :]
                for a in range(3)
            ]
            total = total - (crossed[0] + crossed[1] + crossed[2])
            total = total + closure[pl.ds(c * 4 + y, 16, stride=16), :]
            out[pl.ds(c * 64 + y, 16, stride=4), :] = block[:16] + time_step * total


def call(kernel, shapes, args, scratch=(), scalars=0, flops=0):
    size = 4 * sum(math.prod(s.shape) for s in shapes) + 4 * sum(math.prod(a.shape) for a in args)
    whole = pl.BlockSpec(memory_space=pltpu.VMEM)
    return pl.pallas_call(
        kernel,
        out_shape=shapes,
        in_specs=[pl.BlockSpec(memory_space=pltpu.SMEM)] * scalars
        + [whole] * (len(args) - scalars),
        out_specs=[whole] * len(shapes),
        scratch_shapes=list(scratch),
        compiler_params=pltpu.CompilerParams(vmem_limit_bytes=40 * 2**20),
        cost_estimate=pl.CostEstimate(flops=flops, bytes_accessed=size, transcendentals=0),
    )(*args)


def shape(rows, columns=128, kind=f32):
    return jax.ShapeDtypeStruct((rows, columns), kind)


def body(velocity, cotangent, weight_in, bias_in, weight_out):
    t = {name: jnp.asarray(value) for name, value in constants().items()}
    (modes,) = call(
        transform_z, [shape(512)], [cotangent.reshape(192, 128), t["forward_z"]], flops=4 * 2**22
    )
    planes = lax.all_to_all(modes.reshape(256, 256), ("px", "py"), 0, 0, tiled=True)

    up_x = [(i, (i + 1) % PX) for i in range(PX)]
    down_x = [(b, a) for a, b in up_x]
    up_y = [(i, (i + 1) % PY) for i in range(PY)]
    down_y = [(b, a) for a, b in up_y]
    low = lax.ppermute(velocity[:, 13:].reshape(36, 128), "px", up_x)
    high = lax.ppermute(velocity[:, :3].reshape(36, 128), "px", down_x)
    (own,) = call(extend_x, [shape(288)], [velocity.reshape(192, 128), low, high])
    layers = own.reshape(3, 96, 128)
    low = lax.ppermute(layers[:, 24:].reshape(216, 128), "py", up_y)
    high = lax.ppermute(layers[:, :72].reshape(216, 128), "py", down_y)
    kernel_in = weight_in.reshape(32, 81).T
    kernel_out = weight_out.transpose(0, 2, 3, 4, 1).reshape(162, 32)
    bias = jnp.tile(bias_in, 6).reshape(192, 1)
    field, slope, slants, banded_out, banded_back = call(
        prepare,
        [shape(720), shape(18 * 192), shape(576), shape(192, 3 * STR, bf16), shape(48, 576, bf16)],
        [
            own,
            low,
            high,
            kernel_in,
            kernel_out,
            bias,
            t["select_in"],
            t["select_out"],
            t["select_back"],
        ],
        [pltpu.VMEM((192, 3 * PRE), bf16), pltpu.VMEM((20 * PRE, 128), bf16)],
        flops=18 * 2 * 192 * 256 * 128,
    )

    device = lax.axis_index("px") * PY + lax.axis_index("py")
    which = jnp.stack([device % 2, device // 4]).astype(jnp.int32)
    (returned,) = call(
        project,
        [shape(768)],
        [
            which,
            planes.reshape(512, 128),
            t["row_forward"],
            t["twiddle"],
            t["lane_forward"],
            t["waves"],
            t["lane_backward"],
            t["twiddle_back"],
            t["row_backward"],
        ],
        scalars=1,
        flops=30 * 2 * 256**3,
    )
    received = lax.all_to_all(returned.reshape(256, 384), ("px", "py"), 0, 0, tiled=True)
    (result,) = call(
        finish,
        [shape(192)],
        [
            received.reshape(768, 128),
            t["backward_z"],
            field,
            slope,
            slants,
            banded_out,
            banded_back,
        ],
        [
            pltpu.VMEM((720, 128), f32),
            pltpu.VMEM((48 * 24, 128), f32),
            pltpu.VMEM((20 * STR, 128), bf16),
            pltpu.VMEM((18 * 192, 128), bf16),
            pltpu.VMEM((256, 128), f32),
        ],
        flops=2**29,
    )
    return result.reshape(3, 16, 4, 128)


def solution(mesh):
    placed = (P(None, "px", "py", None), P(None, "px", "py", None), P(), P(), P())
    return jax.shard_map(
        body, mesh=mesh, in_specs=placed, out_specs=P(None, "px", "py", None), check_vma=False
    )
```

profile of v0, /device:TPU:24, one launch (start us, length us, event | category | flops | bytes accessed | tf_op | source)
XLA Modules:
  0.0 98.8 jit_solution(7400024012205100583)
XLA Ops:
  0.0 0.9 copy-done.11
  1.8 0.9 shard_map.163
  2.7 14.4 %all-to-all-start = ((f32[256,1,256]{2,1,0:T(1,128)}), f32[256,1,256]{2,1,0:T(1,128)S(1)}, u32[]{:S(2)}, u32[]{:S(2)}) async-start(f32[256,1,256]{2,1,0:T(1,128)} %bitcast.3), calls=%async_computation | async-start | bytes 524288 | tf_op jit(solution)/shard_map/all_to_all | solution.py:392
  17.3 13.9 %all-to-all-done = f32[256,1,256]{2,1,0:T(1,128)S(1)} async-done(((f32[256,1,256]{2,1,0:T(1,128)}), f32[256,1,256]{2,1,0:T(1,128)S(1)}, u32[]{:S(2)}, u32[]{:S(2)}) %all-to-all-start) | async-done | bytes 262176 | tf_op jit(solution)/shard_map/all_to_all | solution.py:392
  31.2 1.2 %copy-done = bf16[2,2,2,256,256]{4,3,2,1,0:T(8,128)(2,1)S(1)} copy-done((bf16[2,2,2,256,256]{4,3,2,1,0:T(8,128)(2,1)S(1)}, bf16[2,2,2,256,256]{4,3,2,1,0:T(8,128)(2,1)}, u32[]{:S(2)}) %copy-start) | copy-done | bytes 1048600
  32.4 1.0 %copy-done.1 = f32[2,2,256,128]{3,2,1,0:T(8,128)S(1)} copy-done((f32[2,2,256,128]{3,2,1,0:T(8,128)S(1)}, f32[2,2,256,128]{3,2,1,0:T(8,128)}, u32[]{:S(2)}) %copy-start.1) | copy-done | bytes 524312
  33.5 1.0 %copy-done.2 = bf16[2,256,512]{2,1,0:T(8,128)(2,1)S(1)} copy-done((bf16[2,256,512]{2,1,0:T(8,128)(2,1)S(1)}, bf16[2,256,512]{2,1,0:T(8,128)(2,1)}, u32[]{:S(2)}) %copy-start.2) | copy-done | bytes 524312
  34.5 1.0 %copy-done.3 = bf16[2,512,256]{2,1,0:T(8,128)(2,1)S(1)} copy-done((bf16[2,512,256]{2,1,0:T(8,128)(2,1)S(1)}, bf16[2,512,256]{2,1,0:T(8,128)(2,1)}, u32[]{:S(2)}) %copy-start.3) | copy-done | bytes 524312
  35.6 1.0 %copy-done.4 = f32[3,256,128]{2,1,0:T(8,128)S(1)} copy-done((f32[3,256,128]{2,1,0:T(8,128)S(1)}, f32[3,256,128]{2,1,0:T(8,128)}, u32[]{:S(2)}) %copy-start.4) | copy-done | bytes 393240
  36.6 0.9 copy-done.5
  37.5 0.9 copy-done.6
  38.5 3.4 %shard_map.164 = f32[768,128]{1,0:T(8,128)} custom-call(s32[2]{0:T(128)S(1)} %pad_add_fusion.which, f32[512,128]{1,0:T(8,128)S(1)} %bitcast.18, bf16[2,512,256]{2,1,0:T(8,128)(2,1)S(1)} %copy-done.3, f32[2,256,128]{2,1,0:T(8,128)S(1)} %copy-done.6, bf16[2,256,256]{2,1,0:T(8,128)(2,1)S(1)} %copy-done.5, f32[3,256,128]{2,1,0:T(8,128)S(1)} %copy-done.4, ...), custom_call_target="tpu_custom_call" | custom-call | flops 1006632960 | bytes 6553608 | tf_op jit(solution)/shard_map/pallas_call | solution.py:371
  41.8 7.6 %all-to-all-start.1 = ((f32[256,1,384]{2,1,0:T(1,128)}), f32[256,1,384]{2,1,0:T(1,128)S(1)}, u32[]{:S(2)}, u32[]{:S(2)}) async-start(f32[256,1,384]{2,1,0:T(1,128)} %bitcast.5), calls=%async_computation.1 | async-start | bytes 786432 | tf_op jit(solution)/shard_map/all_to_all | solution.py:444
  49.5 6.3 %collective-permute-start = (f32[36,128]{1,0:T(8,128)S(1)}, f32[36,128]{1,0:T(8,128)S(1)}, u32[]{:S(2)}, u32[]{:S(2)}) collective-permute-start(f32[36,128]{1,0:T(8,128)S(1)} %reshape.51), channel_id=1, source_target_pairs={{0,32},{32,64},{64,96},{96,128},{128,160},{160,192},{192,224},{224... | collective-permute-start | bytes 55304 | tf_op jit(solution)/shard_map/ppermute | solution.py:398
  55.9 1.4 %collective-permute-done.low = f32[36,128]{1,0:T(8,128)S(1)} collective-permute-done((f32[36,128]{1,0:T(8,128)S(1)}, f32[36,128]{1,0:T(8,128)S(1)}, u32[]{:S(2)}, u32[]{:S(2)}) %collective-permute-start) | collective-permute-done | bytes 18464 | tf_op jit(solution)/shard_map/ppermute | solution.py:398
  57.3 8.4 %collective-permute-done.1.high = f32[36,128]{1,0:T(8,128)S(1)} collective-permute-done((f32[36,128]{1,0:T(8,128)S(1)}, f32[36,128]{1,0:T(8,128)S(1)}, u32[]{:S(2)}, u32[]{:S(2)}) %collective-permute-start.1) | collective-permute-done | bytes 18464 | tf_op jit(solution)/shard_map/ppermute | solution.py:399
  65.9 5.6 %collective-permute-start.3 = (f32[216,128]{1,0:T(8,128)S(1)}, f32[216,128]{1,0:T(8,128)S(1)}, u32[]{:S(2)}, u32[]{:S(2)}) collective-permute-start(f32[216,128]{1,0:T(8,128)S(1)} %bitcast.22), channel_id=1, source_target_pairs={{1,0},{2,1},{3,2},{4,3},{5,4},{6,5},{7,6},{8,7},{9,8},{10,9},{11,1... | collective-permute-start | bytes 331784 | tf_op jit(solution)/shard_map/ppermute | solution.py:403
  72.3 2.7 %collective-permute-done.2.low = f32[216,128]{1,0:T(8,128)S(1)} collective-permute-done((f32[216,128]{1,0:T(8,128)S(1)}, f32[216,128]{1,0:T(8,128)S(1)}, u32[]{:S(2)}, u32[]{:S(2)}) %collective-permute-start.2) | collective-permute-done | bytes 110624 | tf_op jit(solution)/shard_map/ppermute | solution.py:402
  76.3 0.9 copy-done.9
  77.2 0.9 copy-done.13
  78.1 0.9 copy-done.15
  80.5 5.5 %shard_map.166 = (f32[720,128]{1,0:T(8,128)S(1)}, f32[3456,128]{1,0:T(8,128)S(1)}, f32[576,128]{1,0:T(8,128)S(1)}, bf16[192,432]{1,0:T(8,128)(2,1)S(1)}, bf16[48,576]{1,0:T(8,128)(2,1)S(1)}) custom-call(f32[288,128]{1,0:T(8,128)S(1)} %shard_map.165.own, f32[216,128]{1,0:T(8,128)S(1)} %copy-done.13, f32[216,128]{1,0:T(8,128)S(1)} %copy-done.15, ...), custom_call_target="tpu_custom_call" | custom-call | flops 226492416 | bytes 3913536 | tf_op jit(solution)/shard_map/pallas_call | solution.py:371
  86.7 0.9 copy-done.10
  88.5 10.4 %shard_map.167 = f32[192,128]{1,0:T(8,128)} custom-call(f32[768,128]{1,0:T(8,128)S(1)} %bitcast.17, bf16[2,2,128,128]{3,2,1,0:T(8,128)(2,1)S(1)} %copy-done.10, f32[720,128]{1,0:T(8,128)S(1)} %get-tuple-element.10.field, f32[3456,128]{1,0:T(8,128)S(1)} %get-tuple-element.11.slope, f32[576,128]{1,0:T(8,128)S(1)} %get-tuple-element.12.slants, ...), custom_call_target="tpu_custom_call" | custom-call | flops 536870912 | bytes 3629056 | tf_op jit(solution)/shard_map/pallas_call | solution.py:371
  (50 shorter events, 6.3 us)
Async XLA Ops:
  0.0 0.9 copy-start.11
  0.9 0.9 copy-start.16
  2.7 28.5 %all-to-all-start = ((f32[256,1,256]{2,1,0:T(1,128)}), f32[256,1,256]{2,1,0:T(1,128)S(1)}, u32[]{:S(2)}, u32[]{:S(2)}) async-start(f32[256,1,256]{2,1,0:T(1,128)} %bitcast.3), calls=%async_computation | async-start | bytes 524288 | tf_op jit(solution)/shard_map/all_to_all | solution.py:392
  31.2 1.2 %copy-start = (bf16[2,2,2,256,256]{4,3,2,1,0:T(8,128)(2,1)S(1)}, bf16[2,2,2,256,256]{4,3,2,1,0:T(8,128)(2,1)}, u32[]{:S(2)}) copy-start(bf16[2,2,2,256,256]{4,3,2,1,0:T(8,128)(2,1)} %constant.68.clone.lane_backward) | copy-start | bytes 3145732
  32.4 1.0 %copy-start.1 = (f32[2,2,256,128]{3,2,1,0:T(8,128)S(1)}, f32[2,2,256,128]{3,2,1,0:T(8,128)}, u32[]{:S(2)}) copy-start(f32[2,2,256,128]{3,2,1,0:T(8,128)} %constant.69.clone.twiddle_back) | copy-start | bytes 1572868
  33.5 1.0 %copy-start.2 = (bf16[2,256,512]{2,1,0:T(8,128)(2,1)S(1)}, bf16[2,256,512]{2,1,0:T(8,128)(2,1)}, u32[]{:S(2)}) copy-start(bf16[2,256,512]{2,1,0:T(8,128)(2,1)} %constant.64.clone.row_backward) | copy-start | bytes 1572868
  34.5 1.0 %copy-start.3 = (bf16[2,512,256]{2,1,0:T(8,128)(2,1)S(1)}, bf16[2,512,256]{2,1,0:T(8,128)(2,1)}, u32[]{:S(2)}) copy-start(bf16[2,512,256]{2,1,0:T(8,128)(2,1)} %constant.63.clone.row_forward) | copy-start | bytes 1572868
  35.6 1.0 %copy-start.4 = (f32[3,256,128]{2,1,0:T(8,128)S(1)}, f32[3,256,128]{2,1,0:T(8,128)}, u32[]{:S(2)}) copy-start(f32[3,256,128]{2,1,0:T(8,128)} %constant.67.clone.waves) | copy-start | bytes 1179652
  36.6 0.9 copy-start.5
  37.5 0.9 copy-start.6
  38.5 11.0 %copy-start.8 = (f32[3,16,4,128]{3,2,1,0:T(4,128)S(1)}, f32[3,16,4,128]{3,2,1,0:T(4,128)}, u32[]{:S(2)}) copy-start(f32[3,16,4,128]{3,2,1,0:T(4,128)} %param.17) | copy-start | bytes 294916
  38.5 33.0 %copy-start.22 = (bf16[32,3,3,3,3]{0,4,3,2,1:T(4,128)(2,1)S(1)}, bf16[32,3,3,3,3]{0,4,3,2,1:T(4,128)(2,1)}, u32[]{:S(2)}) copy-start(bf16[32,3,3,3,3]{0,4,3,2,1:T(4,128)(2,1)} %param.19) | copy-start | bytes 15556
  41.8 30.3 %copy-start.21 = (bf16[6,32,3,3,3]{1,4,3,2,0:T(4,128)(2,1)S(1)}, bf16[6,32,3,3,3]{1,4,3,2,0:T(4,128)(2,1)}, u32[]{:S(2)}) copy-start(bf16[6,32,3,3,3]{1,4,3,2,0:T(4,128)(2,1)} %param.21) | copy-start | bytes 31108
  41.8 30.4 %copy-start.23 = (f32[32]{0:T(128)S(1)}, f32[32]{0:T(128)}, u32[]{:S(2)}) copy-start(f32[32]{0:T(128)} %param.20) | copy-start | bytes 388
  41.8 34.5 %copy-start.7 = (bf16[864,81]{1,0:T(8,128)(2,1)S(1)}, bf16[864,81]{1,0:T(8,128)(2,1)}, u32[]{:S(2)}) copy-start(bf16[864,81]{1,0:T(8,128)(2,1)} %constant.72.clone.select_back) | copy-start | bytes 419908
  41.8 44.9 %all-to-all-start.1 = ((f32[256,1,384]{2,1,0:T(1,128)}), f32[256,1,384]{2,1,0:T(1,128)S(1)}, u32[]{:S(2)}, u32[]{:S(2)}) async-start(f32[256,1,384]{2,1,0:T(1,128)} %bitcast.5), calls=%async_computation.1 | async-start | bytes 786432 | tf_op jit(solution)/shard_map/all_to_all | solution.py:444
  49.5 7.8 %collective-permute-start = (f32[36,128]{1,0:T(8,128)S(1)}, f32[36,128]{1,0:T(8,128)S(1)}, u32[]{:S(2)}, u32[]{:S(2)}) collective-permute-start(f32[36,128]{1,0:T(8,128)S(1)} %reshape.51), channel_id=1, source_target_pairs={{0,32},{32,64},{64,96},{96,128},{128,160},{160,192},{192,224},{224... | collective-permute-start | bytes 55304 | tf_op jit(solution)/shard_map/ppermute | solution.py:398
  55.8 9.9 %collective-permute-start.1 = (f32[36,128]{1,0:T(8,128)S(1)}, f32[36,128]{1,0:T(8,128)S(1)}, u32[]{:S(2)}, u32[]{:S(2)}) collective-permute-start(f32[36,128]{1,0:T(8,128)S(1)} %reshape.52), channel_id=1, source_target_pairs={{32,0},{64,32},{96,64},{128,96},{160,128},{192,160},{224,192},{0,2... | collective-permute-start | bytes 55304 | tf_op jit(solution)/shard_map/ppermute | solution.py:399
  65.8 9.2 %collective-permute-start.2 = (f32[216,128]{1,0:T(8,128)S(1)}, f32[216,128]{1,0:T(8,128)S(1)}, u32[]{:S(2)}, u32[]{:S(2)}) collective-permute-start(f32[216,128]{1,0:T(8,128)S(1)} %bitcast.23), channel_id=1, source_target_pairs={{0,1},{1,2},{2,3},{3,4},{4,5},{5,6},{6,7},{7,8},{8,9},{9,10},{10,1... | collective-permute-start | bytes 331784 | tf_op jit(solution)/shard_map/ppermute | solution.py:402
  65.9 9.8 %collective-permute-start.3 = (f32[216,128]{1,0:T(8,128)S(1)}, f32[216,128]{1,0:T(8,128)S(1)}, u32[]{:S(2)}, u32[]{:S(2)}) collective-permute-start(f32[216,128]{1,0:T(8,128)S(1)} %bitcast.22), channel_id=1, source_target_pairs={{1,0},{2,1},{3,2},{4,3},{5,4},{6,5},{7,6},{8,7},{9,8},{10,9},{11,1... | collective-permute-start | bytes 331784 | tf_op jit(solution)/shard_map/ppermute | solution.py:403
  76.3 0.9 copy-start.9
  77.2 0.9 copy-start.13
  78.1 0.9 copy-start.15
  86.7 0.9 copy-start.10
  (6 other events, 4.3 us)
where the time goes:
time: 99.6 us; the launch traced here: 98.8 us
  starting transfers between devices  34.2 us (34%)
  waiting for transfers between devices  26.4 us (27%)
  Pallas kernels  20.2 us (20%)
  local copies, waits for them, and re-layouts  17.8 us (18%)
    pallas_call x5, Pallas kernels, call(): pl.pallas_call(kernel, out_shape=shapes, in_specs=[pl.BlockSpec(memory_sp...  20.2 us
    unnamed x48, local copies, waits for them, and re-layouts  16.9 us
    all_to_all x1, starting transfers between devices, body(): lax.all_to_all(modes.reshape(256, 256), ('px', 'py'), 0, 0, tiled=True)  14.4 us
    all_to_all x1, waiting for transfers between devices, body(): lax.all_to_all(modes.reshape(256, 256), ('px', 'py'), 0, 0, tiled=True)  13.9 us
    ppermute x1, waiting for transfers between devices, body(): high = lax.ppermute(velocity[:, :3].reshape(36, 128), 'px', down_x)  8.44 us
    all_to_all x1, starting transfers between devices, body(): lax.all_to_all(returned.reshape(256, 384), ('px', 'py'), 0, 0, tiled=True)  7.6 us
    ppermute x1, starting transfers between devices, body(): low = lax.ppermute(velocity[:, 13:].reshape(36, 128), 'px', up_x)  6.32 us
    ppermute x1, starting transfers between devices, body(): high = lax.ppermute(layers[:, :72].reshape(216, 128), 'py', down_y)  5.64 us
  transfers between devices with their start and end apart: 6, of which 4 were waited for; matrix products, arithmetic and copies ran while one was open for 1% of the time, Pallas kernels for 6%

commit v1 on v0

--- a/solution.py
+++ b/solution.py
@@ -17,6 +17,8 @@
 spacing = 2.0 * math.pi / N
 bf16 = jnp.bfloat16
 f32 = jnp.float32
+FULL = 60 * 2**20
+MOST = 2**26 - 9 * 2**15
 PRE = 80
 STR = 144
 
@@ -133,7 +135,16 @@
     return one(left[0], right[0]) + (one(left[1], right[0]) + one(left[0], right[1]))
 
 
-def transform_z(source, table, out):
+def fetch(pairs, sems):
+    copies = [pltpu.make_async_copy(a, b, sems.at[i]) for i, (a, b) in enumerate(pairs)]
+    for copy in copies:
+        copy.start()
+    return copies
+
+
+def transform_z(source_far, table_far, out, source, table, sems):
+    for copy in fetch([(source_far, source), (table_far, table)], sems):
+        copy.wait()
     blocks = [[source[pl.ds(c * 64 + y, 16, stride=4), :] for y in range(4)] for c in range(3)]
     first = jnp.concatenate(blocks[0] + blocks[1], 0)
     second = jnp.concatenate(blocks[2] + blocks[2], 0)
@@ -144,7 +155,15 @@
 
 
 def project(
-    which,
+    source_far,
+    row_forward_far,
+    twiddle_far,
+    lane_forward_far,
+    waves_far,
+    lane_backward_far,
+    twiddle_back_far,
+    row_backward_far,
+    out,
     source,
     row_forward,
     twiddle,
@@ -153,12 +172,30 @@
     lane_backward,
     twiddle_back,
     row_backward,
-    out,
+    sems,
 ):
-    part = which[0]
-    kz = which[1].astype(f32)
+    device = lax.axis_index("px") * PY + lax.axis_index("py")
+    part = lax.rem(device, 2)
+    kz = lax.div(device, 4).astype(f32)
+    first, *copies = fetch(
+        [
+            (source_far, source),
+            (row_forward_far, row_forward),
+            (twiddle_far, twiddle),
+            (lane_forward_far, lane_forward),
+            (waves_far, waves),
+            (lane_backward_far.at[part], lane_backward),
+            (twiddle_back_far.at[part], twiddle_back),
+            (row_backward_far, row_backward),
+        ],
+        sems,
+    )
+    first.wait()
+    copies[0].wait()
     tiles = [source[pl.ds(tile, 256, stride=2), :] for tile in range(2)]
     mixed = product((row_forward[0], row_forward[1]), split(jnp.concatenate(tiles, 1)))
+    copies[1].wait()
+    copies[2].wait()
     cos, sin = twiddle[0], twiddle[1]
     spectrum = []
     for tile in range(2):
@@ -166,6 +203,7 @@
         imag = mixed[256:, tile * 128 : tile * 128 + 128]
         turned = jnp.concatenate([real * cos - imag * sin, real * sin + imag * cos], 1)
         spectrum.append(product(split(turned), (lane_forward[0], lane_forward[1])))
+    copies[3].wait()
     wave, square, retain = waves[0], waves[1], waves[2]
     inverse = 1.0 / jnp.maximum(square + kz * kz, 1.0)
     (hr, hi), (vr, vi) = [(s[:, :128], s[:, 128:]) for s in spectrum]
@@ -177,13 +215,16 @@
     flat = jnp.concatenate([(hr - wave * dot_r) * retain, (hi - wave * dot_i) * retain], 1)
     upright = jnp.concatenate([(vr + kz * dot_i) * retain, (vi - kz * dot_r) * retain], 1)
     flat, upright = split(flat), split(upright)
-    cos, sin = twiddle_back[part, 0], twiddle_back[part, 1]
+    copies[4].wait()
+    copies[5].wait()
+    cos, sin = twiddle_back[0], twiddle_back[1]
     parts = []
     for component in range(3):
-        matrix = lane_backward.at[part, component % 2]
+        matrix = lane_backward.at[component % 2]
         cells = product(upright if component == 2 else flat, (matrix[0], matrix[1]))
         real, imag = cells[:, :128], cells[:, 128:]
         parts.append(jnp.concatenate([real * cos - imag * sin, real * sin + imag * cos], 0))
+    copies[6].wait()
     result = product((row_backward[0], row_backward[1]), split(jnp.concatenate(parts, 1)))
     for component in range(3):
         block = result[:, component * 128 : component * 128 + 128]
@@ -209,60 +250,55 @@
     return lambda k: pltpu.roll(block, (-k) % block.shape[axis], axis)
 
 
-def prepare(
-    own,
-    low,
-    high,
+def band_weights(
     kernel_in,
     kernel_out,
-    bias,
     select_in,
     select_out,
     select_back,
-    field,
-    slope,
-    slants,
+    banded_in,
     banded_out,
     banded_back,
-    banded_in,
-    slabs,
 ):
-    for c in range(3):
-        field[pl.ds(c * 240, 72), :] = low[pl.ds(c * 72, 72), :]
-        field[pl.ds(c * 240 + 72, 96), :] = own[pl.ds(c * 96, 96), :]
-        field[pl.ds(c * 240 + 168, 72), :] = high[pl.ds(c * 72, 72), :]
     over_rows = (((0,), (0,)), ((), ()))
-    band = lax.dot_general(kernel_in[...], select_in[...], over_rows, preferred_element_type=f32)
-    for yo in range(6):
-        moved = band if yo == 0 else jnp.concatenate([jnp.zeros((32, yo), f32), band[:, :-yo]], 1)
-        banded_in[pl.ds(yo * 32, 32), :] = moved.astype(bf16)
-    band = lax.dot_general(kernel_out[...], select_out[...], over_rows, preferred_element_type=f32)
-    for yo in range(6):
-        moved = band if yo == 0 else jnp.concatenate([jnp.zeros((32, yo), f32), band[:, :-yo]], 1)
-        banded_out[pl.ds(yo * 32, 32), :] = moved.astype(bf16)
+    for kernel, select, banded in (
+        (kernel_in, select_in, banded_in),
+        (kernel_out, select_out, banded_out),
+    ):
+        band = lax.dot_general(kernel[...], select[...], over_rows, preferred_element_type=f32)
+        for yo in range(6):
+            moved = band
+            if yo:
+                moved = jnp.concatenate([jnp.zeros((32, yo), f32), band[:, :-yo]], 1)
+            banded[pl.ds(yo * 32, 32), :] = moved.astype(bf16)
     band = jnp.dot(select_back[...], kernel_in[...], preferred_element_type=f32).astype(bf16)
     for block in range(18):
         banded_back[:, pl.ds(block * 32, 32)] = band[block * 48 : block * 48 + 48]
 
-    def gather(i, carry):
-        row = lax.rem(i + 22, 24)
+
+def prepare(own, low, high, bias, banded_in, field, slope, slants, slabs, sems):
+    pairs = []
+    for c in range(3):
+        for source, start, rows in ((low, 0, 72), (own, 72, 96), (high, 168, 72)):
+            target = field.at[pl.ds(c * 240 + start, rows), :]
+            pairs.append((source.at[pl.ds(c * rows, rows), :], target))
+    for copy in fetch(pairs, sems):
+        copy.wait()
+
+    for i in range(20):
+        row = (i + 22) % 24
         parts = [field[pl.ds(c * 240 + 24 + row, 8, stride=24), :] for c in range(3)]
         slab = jnp.concatenate(parts, 0)
         shifts = [pltpu.roll(slab, 1, 1), slab, pltpu.roll(slab, 127, 1)]
-        slab = jnp.concatenate(shifts + [jnp.zeros((8, 128), f32)], 0)
-        slabs[pl.ds(pl.multiple_of(i * PRE, 16), PRE), :] = slab.astype(bf16)
-        return carry
-
-    lax.fori_loop(0, 20, gather, 0)
-
-    def activate(i, carry):
-        cells = slabs[pl.ds(pl.multiple_of(i * PRE, 16), 3 * PRE), :]
+        slab = jnp.concatenate(shifts + [jnp.zeros((8, 128), f32)], 0).astype(bf16)
+        for half, j in enumerate((i, i - 9)):
+            if 0 <= j <= 10:
+                slabs[pl.ds(j * PRE, PRE), pl.ds(half * 128, 128)] = slab
+    for i in range(9):
+        cells = slabs[pl.ds(i * PRE, 3 * PRE), :]
         value = jnp.dot(banded_in[...], cells, preferred_element_type=f32) + bias[...]
         value = jnp.tanh(value)
-        slope[pl.ds(pl.multiple_of(i * 192, 8), 192), :] = 1.0 - value * value
-        return carry
-
-    lax.fori_loop(0, 18, activate, 0)
+        slope[pl.ds(i * 192, 192), :] = 1.0 - value * value
     for a in range(3):
         for y in range(4):
             base = a * 240 + (y + 3) * 24
@@ -278,20 +314,42 @@
 
 
 def finish(
+    modes_far,
+    table_far,
+    field_far,
+    slants_far,
+    slope_far,
+    banded_out_far,
+    banded_back_far,
+    out,
     modes,
     table,
     field,
+    slants,
     slope,
-    slants,
     banded_out,
     banded_back,
-    out,
     lam,
     stress,
     slabs,
     adjoint,
     closure,
+    sems,
 ):
+    copies = fetch(
+        [
+            (modes_far, modes),
+            (table_far, table),
+            (banded_out_far, banded_out),
+            (slope_far, slope),
+            (banded_back_far, banded_back),
+            (field_far, field),
+            (slants_far, slants),
+        ],
+        sems,
+    )
+    copies[0].wait()
+    copies[1].wait()
     for c in range(3):
         matrix = table.at[c // 2]
         for part in range(2):
@@ -317,34 +375,33 @@
         ]
         for s in range(6):
             stress[pl.ds((s * 8 + y) * 24, 24), :] = values[s]
-
-    def gather(i, carry):
-        row = lax.rem(i + 22, 24)
-        slab = stress[pl.ds(row, 48, stride=24), :]
+    for i in range(20):
+        slab = stress[pl.ds((i + 22) % 24, 48, stride=24), :]
         shifts = [pltpu.roll(slab, 1, 1), slab, pltpu.roll(slab, 127, 1)]
-        slab = jnp.concatenate(shifts, 0)
-        slabs[pl.ds(pl.multiple_of(i * STR, 16), STR), :] = slab.astype(bf16)
-        return carry
-
-    lax.fori_loop(0, 20, gather, 0)
-
-    def hidden(i, carry):
-        cells = slabs[pl.ds(pl.multiple_of(i * STR, 16), 3 * STR), :]
+        slab = jnp.concatenate(shifts, 0).astype(bf16)
+        for half, j in enumerate((i, i - 9)):
+            if 0 <= j <= 10:
+                slabs[pl.ds(j * STR, STR), pl.ds(half * 128, 128)] = slab
+    copies[2].wait()
+    copies[3].wait()
+    for i in range(9):
+        cells = slabs[pl.ds(i * STR, 3 * STR), :]
         value = jnp.dot(banded_out[...], cells, preferred_element_type=f32)
-        rows = pl.ds(pl.multiple_of(i * 192, 16), 192)
-        adjoint[rows, :] = (value * slope[rows, :]).astype(bf16)
-        return carry
-
-    lax.fori_loop(0, 18, hidden, 0)
-
-    def back(i, carry):
-        cells = adjoint[pl.ds(pl.multiple_of(i * 192, 16), 576), :]
+        value = (value * slope[pl.ds(i * 192, 192), :]).astype(bf16)
+        for x, block in ((i, value[:, :128]), (i + 9, value[:, 128:])):
+            for half, j in enumerate((x, x - 8)):
+                if 0 <= j <= 9:
+                    adjoint[pl.ds(j * 192, 192), pl.ds(half * 128, 128)] = block
+    copies[4].wait()
+    for i in range(8):
+        cells = adjoint[pl.ds(i * 192, 576), :]
         value = jnp.dot(banded_back[...], cells, preferred_element_type=f32)
-        total = value[16:32] + pltpu.roll(value[:16], 127, 1) + pltpu.roll(value[32:], 1, 1)
-        closure[pl.ds(pl.multiple_of(i * 16, 16), 16), :] = total
-        return carry
-
-    lax.fori_loop(0, 16, back, 0)
+        for half in range(2):
+            block = value[:, half * 128 : half * 128 + 128]
+            total = block[16:32] + pltpu.roll(block[:16], 127, 1) + pltpu.roll(block[32:], 1, 1)
+            closure[pl.ds((i + 8 * half) * 16, 16), :] = total
+    copies[5].wait()
+    copies[6].wait()
     for c in range(3):
         across = [
             lam[pl.ds(c * 240 + y * 24, 16), :] * field[pl.ds(240 + y * 24, 16), :]
@@ -365,17 +422,17 @@
             out[pl.ds(c * 64 + y, 16, stride=4), :] = block[:16] + time_step * total
 
 
-def call(kernel, shapes, args, scratch=(), scalars=0, flops=0):
+def call(kernel, shapes, args, spaces, scratch=(), copies=0, limit=24 * 2**20, flops=0):
     size = 4 * sum(math.prod(s.shape) for s in shapes) + 4 * sum(math.prod(a.shape) for a in args)
-    whole = pl.BlockSpec(memory_space=pltpu.VMEM)
+    kinds = {"v": pltpu.VMEM, "s": pltpu.SMEM, "h": pltpu.HBM}
+    scratch = list(scratch) + ([pltpu.SemaphoreType.DMA((copies,))] if copies else [])
     return pl.pallas_call(
         kernel,
         out_shape=shapes,
-        in_specs=[pl.BlockSpec(memory_space=pltpu.SMEM)] * scalars
-        + [whole] * (len(args) - scalars),
-        out_specs=[whole] * len(shapes),
-        scratch_shapes=list(scratch),
-        compiler_params=pltpu.CompilerParams(vmem_limit_bytes=40 * 2**20),
+        in_specs=[pl.BlockSpec(memory_space=kinds[space]) for space in spaces],
+        out_specs=[pl.BlockSpec(memory_space=pltpu.VMEM)] * len(shapes),
+        scratch_shapes=scratch,
+        compiler_params=pltpu.CompilerParams(vmem_limit_bytes=limit),
         cost_estimate=pl.CostEstimate(flops=flops, bytes_accessed=size, transcendentals=0),
     )(*args)
 
@@ -387,9 +444,20 @@
 def body(velocity, cotangent, weight_in, bias_in, weight_out):
     t = {name: jnp.asarray(value) for name, value in constants().items()}
     (modes,) = call(
-        transform_z, [shape(512)], [cotangent.reshape(192, 128), t["forward_z"]], flops=4 * 2**22
+        transform_z,
+        [shape(512)],
+        [cotangent.reshape(192, 128), t["forward_z"]],
+        "hh",
+        [pltpu.VMEM((192, 128), f32), pltpu.VMEM((2, 2, 128, 128), bf16)],
+        2,
+        limit=FULL,
+        flops=4 * 2**22,
+    )
+    modes, velocity, weight_in, bias_in, weight_out = lax.optimization_barrier(
+        (modes, velocity, weight_in, bias_in, weight_out)
     )
     planes = lax.all_to_all(modes.reshape(256, 256), ("px", "py"), 0, 0, tiled=True)
+    planes = planes.reshape(512, 128)
 
     up_x = [(i, (i + 1) % PX) for i in range(PX)]
     down_x = [(b, a) for a, b in up_x]
@@ -397,70 +465,79 @@
     down_y = [(b, a) for a, b in up_y]
     low = lax.ppermute(velocity[:, 13:].reshape(36, 128), "px", up_x)
     high = lax.ppermute(velocity[:, :3].reshape(36, 128), "px", down_x)
-    (own,) = call(extend_x, [shape(288)], [velocity.reshape(192, 128), low, high])
+    (own,) = call(extend_x, [shape(288)], [velocity.reshape(192, 128), low, high], "vvv")
+    kernel_in = weight_in.reshape(32, 81).T
+    kernel_out = weight_out.transpose(0, 2, 3, 4, 1).reshape(162, 32)
+    banded_in, banded_out, banded_back = call(
+        band_weights,
+        [shape(192, 3 * PRE, bf16), shape(192, 3 * STR, bf16), shape(48, 576, bf16)],
+        [kernel_in, kernel_out, t["select_in"], t["select_out"], t["select_back"]],
+        "vvvvv",
+        flops=2**27,
+    )
+    bias = jnp.tile(bias_in, 6).reshape(192, 1)
+    planes, own, bias, banded_in, banded_out, banded_back = lax.optimization_barrier(
+        (planes, own, bias, banded_in, banded_out, banded_back)
+    )
+    tables = [
+        t["row_forward"],
+        t["twiddle"],
+        t["lane_forward"],
+        t["waves"],
+        t["lane_backward"],
+        t["twiddle_back"],
+        t["row_backward"],
+    ]
+    picked = {4: 1, 5: 1}
+    (returned,) = call(
+        project,
+        [shape(768)],
+        [planes] + tables,
+        "h" * 8,
+        [pltpu.VMEM((512, 128), f32)]
+        + [pltpu.VMEM(a.shape[picked.get(i, 0) :], a.dtype) for i, a in enumerate(tables)],
+        8,
+        limit=MOST,
+        flops=30 * 2 * 256**3,
+    )
+    received = lax.all_to_all(returned.reshape(256, 384), ("px", "py"), 0, 0, tiled=True)
     layers = own.reshape(3, 96, 128)
     low = lax.ppermute(layers[:, 24:].reshape(216, 128), "py", up_y)
     high = lax.ppermute(layers[:, :72].reshape(216, 128), "py", down_y)
-    kernel_in = weight_in.reshape(32, 81).T
-    kernel_out = weight_out.transpose(0, 2, 3, 4, 1).reshape(162, 32)
-    bias = jnp.tile(bias_in, 6).reshape(192, 1)
-    field, slope, slants, banded_out, banded_back = call(
+    field, slope, slants = call(
         prepare,
-        [shape(720), shape(18 * 192), shape(576), shape(192, 3 * STR, bf16), shape(48, 576, bf16)],
-        [
-            own,
-            low,
-            high,
-            kernel_in,
-            kernel_out,
-            bias,
-            t["select_in"],
-            t["select_out"],
-            t["select_back"],
-        ],
-        [pltpu.VMEM((192, 3 * PRE), bf16), pltpu.VMEM((20 * PRE, 128), bf16)],
+        [shape(720), shape(9 * 192, 256), shape(576)],
+        [own, low, high, bias, banded_in],
+        "hhhvv",
+        [pltpu.VMEM((11 * PRE, 256), bf16)],
+        9,
+        limit=FULL,
         flops=18 * 2 * 192 * 256 * 128,
     )
-
-    device = lax.axis_index("px") * PY + lax.axis_index("py")
-    which = jnp.stack([device % 2, device // 4]).astype(jnp.int32)
-    (returned,) = call(
-        project,
-        [shape(768)],
-        [
-            which,
-            planes.reshape(512, 128),
-            t["row_forward"],
-            t["twiddle"],
-            t["lane_forward"],
-            t["waves"],
-            t["lane_backward"],
-            t["twiddle_back"],
-            t["row_backward"],
-        ],
-        scalars=1,
-        flops=30 * 2 * 256**3,
-    )
-    received = lax.all_to_all(returned.reshape(256, 384), ("px", "py"), 0, 0, tiled=True)
+    operands = [
+        received.reshape(768, 128),
+        t["backward_z"],
+        field,
+        slants,
+        slope,
+        banded_out,
+        banded_back,
+    ]
     (result,) = call(
         finish,
         [shape(192)],
-        [
-            received.reshape(768, 128),
-            t["backward_z"],
-            field,
-            slope,
-            slants,
-            banded_out,
-            banded_back,
-        ],
-        [
+        operands,
+        "h" * 7,
+        [pltpu.VMEM(a.shape, a.dtype) for a in operands]
+        + [
             pltpu.VMEM((720, 128), f32),
             pltpu.VMEM((48 * 24, 128), f32),
-            pltpu.VMEM((20 * STR, 128), bf16),
-            pltpu.VMEM((18 * 192, 128), bf16),
+            pltpu.VMEM((11 * STR, 256), bf16),
+            pltpu.VMEM((10 * 192, 256), bf16),
             pltpu.VMEM((256, 128), f32),
         ],
+        7,
+        limit=MOST,
         flops=2**29,
     )
     return result.reshape(3, 16, 4, 128)

time: 99.6 us -> 75.1 us (0.75)
  waiting for transfers between devices: 26.4 us -> 10.1 us
  local copies, waits for them, and re-layouts: 17.8 us -> 9.76 us
  Pallas kernels: 20.2 us -> 14.9 us
  starting transfers between devices: 34.2 us -> 39.4 us
    all_to_all x1, waiting for transfers between devices: 13.9 us -> 0.01 us  [body(): lax.all_to_all(modes.reshape(256, 256), ('px', 'py'), 0, 0, tiled=True)]
    unnamed x48 -> x20, local copies, waits for them, and re-layouts: 16.9 us -> 5.84 us
    ppermute x1, waiting for transfers between devices: 8.44 us -> 2.45 us  [body(): high = lax.ppermute(velocity[:, :3].reshape(36, 128), 'px', down_x)]
    pallas_call x5 -> x6, Pallas kernels: 20.2 us -> 14.9 us  [call(): pl.pallas_call(kernel, out_shape=shapes, in_specs=[pl.BlockSpec(memory_sp...]
    ppermute x1, waiting for transfers between devices: 2.68 us -> 7.69 us  [body(): low = lax.ppermute(layers[:, 24:].reshape(216, 128), 'py', up_y)]
    all_to_all x1, starting transfers between devices: 7.6 us -> 11.4 us  [body(): lax.all_to_all(returned.reshape(256, 384), ('px', 'py'), 0, 0, tiled=True)]
    ppermute x1, waiting for transfers between devices: 1.38 us -> 0.01 us  [body(): low = lax.ppermute(velocity[:, 13:].reshape(36, 128), 'px', up_x)]
    all_to_all x1, starting transfers between devices: 14.4 us -> 15.4 us  [body(): lax.all_to_all(modes.reshape(256, 256), ('px', 'py'), 0, 0, tiled=True)]
  transfers between devices with their start and end apart: 6 -> 6, of which waited for: 4 -> 2; matrix products, arithmetic and copies ran while one was open for 1% -> 5% of each run, Pallas kernels for 6% -> 6%
where the time goes in v1:
time: 75.1 us; the launch traced here: 74.3 us
  starting transfers between devices  39.4 us (52%)
  Pallas kernels  14.9 us (20%)
  waiting for transfers between devices  10.1 us (13%)
  local copies, waits for them, and re-layouts  9.76 us (13%)
    all_to_all x1, starting transfers between devices, body(): lax.all_to_all(modes.reshape(256, 256), ('px', 'py'), 0, 0, tiled=True)  15.4 us
    pallas_call x6, Pallas kernels, call(): pl.pallas_call(kernel, out_shape=shapes, in_specs=[pl.BlockSpec(memory_sp...  14.9 us
    all_to_all x1, starting transfers between devices, body(): lax.all_to_all(returned.reshape(256, 384), ('px', 'py'), 0, 0, tiled=True)  11.4 us
    ppermute x1, waiting for transfers between devices, body(): low = lax.ppermute(layers[:, 24:].reshape(216, 128), 'py', up_y)  7.69 us
    ppermute x1, starting transfers between devices, body(): low = lax.ppermute(velocity[:, 13:].reshape(36, 128), 'px', up_x)  6.32 us
    ppermute x1, starting transfers between devices, body(): high = lax.ppermute(layers[:, :72].reshape(216, 128), 'py', down_y)  5.92 us
    unnamed x20, local copies, waits for them, and re-layouts  5.84 us
    ppermute x1, waiting for transfers between devices, body(): high = lax.ppermute(velocity[:, :3].reshape(36, 128), 'px', down_x)  2.45 us
  transfers between devices with their start and end apart: 6, of which 2 were waited for; matrix products, arithmetic and copies ran while one was open for 5% of the time, Pallas kernels for 6%

profile of v1, /device:TPU:24, one launch (start us, length us, event | category | flops | bytes accessed | tf_op | source)
XLA Modules:
  0.0 74.3 jit_solution(17256435616563485795)
XLA Ops:
  0.0 2.0 %shard_map.163 = f32[512,128]{1,0:T(8,128)} custom-call(f32[192,128]{1,0:T(8,128)} %bitcast.21, bf16[2,2,128,128]{3,2,1,0:T(8,128)(2,1)} %constant.24.clone.table_far), custom_call_target="tpu_custom_call" | custom-call | flops 16777216 | bytes 622592 | tf_op jit(solution)/shard_map/pallas_call | solution.py:429
  2.0 15.4 %all-to-all-start = ((f32[256,1,256]{2,1,0:T(1,128)}), f32[256,1,256]{2,1,0:T(1,128)}, u32[]{:S(2)}, u32[]{:S(2)}) async-start(f32[256,1,256]{2,1,0:T(1,128)} %bitcast.18), calls=%async_computation | async-start | bytes 524288 | tf_op jit(solution)/shard_map/all_to_all | solution.py:459
  17.4 0.8 %fusion.1 = (f32[3,3,4,128]{3,2,1,0:T(4,128)S(1)}, f32[3,3,4,128]{3,2,1,0:T(4,128)S(1)}) fusion(f32[3,16,4,128]{3,2,1,0:T(4,128)} %param.17), kind=kLoop, calls=%fused_computation.1 | loop fusion | bytes 73728 | tf_op jit(solution)/shard_map/slice | solution.py:467
  18.2 6.3 %collective-permute-start = (f32[36,128]{1,0:T(8,128)S(1)}, f32[36,128]{1,0:T(8,128)S(1)}, u32[]{:S(2)}, u32[]{:S(2)}) collective-permute-start(f32[36,128]{1,0:T(8,128)S(1)} %reshape.50), channel_id=1, source_target_pairs={{0,32},{32,64},{64,96},{96,128},{128,160},{160,192},{192,224},{224... | collective-permute-start | bytes 55304 | tf_op jit(solution)/shard_map/ppermute | solution.py:466
  24.6 0.9 %reshape.53.kernel_out = bf16[162,32]{1,0:T(8,128)(2,1)S(1)} reshape(bf16[6,3,3,3,32]{4,3,2,1,0:T(4,128)(2,1)} %bitcast.22) | data formatting | bytes 20736 | tf_op jit(solution)/shard_map/reshape | solution.py:470
  25.5 0.8 %reshape.52 = bf16[32,81]{0,1:T(8,128)(2,1)S(1)} reshape(bf16[32,3,3,3,3]{0,4,3,2,1:T(4,128)(2,1)} %param.19) | data formatting | bytes 10368 | tf_op jit(solution)/shard_map/reshape | solution.py:469
  26.2 0.7 tile.2
  27.0 0.9 %copy-done.1 = bf16[864,81]{1,0:T(8,128)(2,1)S(1)} copy-done((bf16[864,81]{1,0:T(8,128)(2,1)S(1)}, bf16[864,81]{1,0:T(8,128)(2,1)}, u32[]{:S(2)}) %copy-start.1) | copy-done | bytes 139992
  27.9 0.9 %copy-done.4 = bf16[162,432]{1,0:T(8,128)(2,1)S(1)} copy-done((bf16[162,432]{1,0:T(8,128)(2,1)S(1)}, bf16[162,432]{1,0:T(8,128)(2,1)}, u32[]{:S(2)}) %copy-start.4) | copy-done | bytes 139992
  28.8 0.8 %copy-done.6 = bf16[81,240]{1,0:T(8,128)(2,1)S(1)} copy-done((bf16[81,240]{1,0:T(8,128)(2,1)S(1)}, bf16[81,240]{1,0:T(8,128)(2,1)}, u32[]{:S(2)}) %copy-start.6) | copy-done | bytes 38904
  29.6 0.4 shard_map.165
  30.0 0.7 copy-done.2
  30.7 0.6 copy-done.5
  31.3 0.6 copy-done.7
  31.9 2.4 %collective-permute-done.1.high = f32[36,128]{1,0:T(8,128)S(1)} collective-permute-done((f32[36,128]{1,0:T(8,128)S(1)}, f32[36,128]{1,0:T(8,128)S(1)}, u32[]{:S(2)}, u32[]{:S(2)}) %collective-permute-start.1) | collective-permute-done | bytes 18464 | tf_op jit(solution)/shard_map/ppermute | solution.py:467
  34.4 4.5 %shard_map.166 = f32[768,128]{1,0:T(8,128)} custom-call(f32[512,128]{1,0:T(8,128)} %bitcast.2.source_far, bf16[2,512,256]{2,1,0:T(8,128)(2,1)} %constant.26.clone.row_forward_far, f32[2,256,128]{2,1,0:T(8,128)} %constant.28.clone.twiddle_far, bf16[2,256,256]{2,1,0:T(8,128)(2,1)} %constant.29.clone.lane_forward_far, f32[3,256,128]{2,1,0:T(8,128)} %constant.30.clone.waves_far, ...), custom_call_target="tpu_custom_call" | custom-call | flops 1006632960 | bytes 6553600 | tf_op jit(solution)/shard_map/pallas_call | solution.py:429
  39.0 11.4 %all-to-all-start.1 = ((f32[256,1,384]{2,1,0:T(1,128)}), f32[256,1,384]{2,1,0:T(1,128)}, u32[]{:S(2)}, u32[]{:S(2)}) async-start(f32[256,1,384]{2,1,0:T(1,128)} %bitcast.17), calls=%async_computation.1 | async-start | bytes 786432 | tf_op jit(solution)/shard_map/all_to_all | solution.py:503
  50.6 5.9 %collective-permute-start.3 = (f32[216,128]{1,0:T(8,128)S(1)}, f32[216,128]{1,0:T(8,128)S(1)}, u32[]{:S(2)}, u32[]{:S(2)}) collective-permute-start(f32[216,128]{1,0:T(8,128)S(1)} %bitcast.19), channel_id=1, source_target_pairs={{1,0},{2,1},{3,2},{4,3},{5,4},{6,5},{7,6},{8,7},{9,8},{10,9},{11,1... | collective-permute-start | bytes 331784 | tf_op jit(solution)/shard_map/ppermute | solution.py:506
  56.6 0.8 %copy.21.bias = f32[192,1]{1,0:T(8,128)} copy(f32[192,1]{0,1:T(1,128)S(1)} %reshape_tile.3) | data formatting | bytes 1536 | tf_op jit(solution)/shard_map/optimization_barrier | solution.py:479
  57.3 7.7 %collective-permute-done.2.low = f32[216,128]{1,0:T(8,128)S(1)} collective-permute-done((f32[216,128]{1,0:T(8,128)S(1)}, f32[216,128]{1,0:T(8,128)S(1)}, u32[]{:S(2)}, u32[]{:S(2)}) %collective-permute-start.2) | collective-permute-done | bytes 110624 | tf_op jit(solution)/shard_map/ppermute | solution.py:505
  65.0 0.6 copy-done.8
  65.6 0.6 copy-done.9
  66.3 3.9 %shard_map.167 = (f32[720,128]{1,0:T(8,128)}, f32[1728,256]{1,0:T(8,128)}, f32[576,128]{1,0:T(8,128)}) custom-call(f32[288,128]{1,0:T(8,128)} %copy-done, f32[216,128]{1,0:T(8,128)} %copy-done.8, f32[216,128]{1,0:T(8,128)} %copy-done.9, f32[192,1]{1,0:T(8,128)} %copy.21.bias, bf16[192,240]{1,0:T(8,128)(2,1)} %copy-done.7), custom_call_target="tpu_custom_call" | custom-call | flops 226492416 | bytes 2986752 | tf_op jit(solution)/shard_map/pallas_call | solution.py:429
  70.2 4.1 %shard_map.168 = f32[192,128]{1,0:T(8,128)} custom-call(f32[768,128]{1,0:T(8,128)} %bitcast.7.modes_far, bf16[2,2,128,128]{3,2,1,0:T(8,128)(2,1)} %constant.25.clone.table_far, f32[720,128]{1,0:T(8,128)} %get-tuple-element.34.field_far, f32[576,128]{1,0:T(8,128)} %get-tuple-element.35.slants_far, f32[1728,256]{1,0:T(8,128)} %get-tuple-element.36.slope_far, ...), custom_call_target="tpu_custom_call" | custom-call | flops 536870912 | bytes 3629056 | tf_op jit(solution)/shard_map/pallas_call | solution.py:429
  (23 shorter events, 0.5 us)
Async XLA Ops:
  0.0 34.4 %copy-start.3 = (f32[3,16,4,128]{3,2,1,0:T(4,128)S(1)}, f32[3,16,4,128]{3,2,1,0:T(4,128)}, u32[]{:S(2)}) copy-start(f32[3,16,4,128]{3,2,1,0:T(4,128)} %param.17) | copy-start | bytes 294916
  2.0 32.5 %all-to-all-start = ((f32[256,1,256]{2,1,0:T(1,128)}), f32[256,1,256]{2,1,0:T(1,128)}, u32[]{:S(2)}, u32[]{:S(2)}) async-start(f32[256,1,256]{2,1,0:T(1,128)} %bitcast.18), calls=%async_computation | async-start | bytes 524288 | tf_op jit(solution)/shard_map/all_to_all | solution.py:459
  18.2 13.8 %collective-permute-start = (f32[36,128]{1,0:T(8,128)S(1)}, f32[36,128]{1,0:T(8,128)S(1)}, u32[]{:S(2)}, u32[]{:S(2)}) collective-permute-start(f32[36,128]{1,0:T(8,128)S(1)} %reshape.50), channel_id=1, source_target_pairs={{0,32},{32,64},{64,96},{96,128},{128,160},{160,192},{192,224},{224... | collective-permute-start | bytes 55304 | tf_op jit(solution)/shard_map/ppermute | solution.py:466
  24.5 9.9 %collective-permute-start.1 = (f32[36,128]{1,0:T(8,128)S(1)}, f32[36,128]{1,0:T(8,128)S(1)}, u32[]{:S(2)}, u32[]{:S(2)}) collective-permute-start(f32[36,128]{1,0:T(8,128)S(1)} %reshape.51), channel_id=1, source_target_pairs={{32,0},{64,32},{96,64},{128,96},{160,128},{192,160},{224,192},{0,2... | collective-permute-start | bytes 55304 | tf_op jit(solution)/shard_map/ppermute | solution.py:467
  27.0 0.9 %copy-start.1 = (bf16[864,81]{1,0:T(8,128)(2,1)S(1)}, bf16[864,81]{1,0:T(8,128)(2,1)}, u32[]{:S(2)}) copy-start(bf16[864,81]{1,0:T(8,128)(2,1)} %constant.35.clone.select_back) | copy-start | bytes 419908
  27.9 0.9 %copy-start.4 = (bf16[162,432]{1,0:T(8,128)(2,1)S(1)}, bf16[162,432]{1,0:T(8,128)(2,1)}, u32[]{:S(2)}) copy-start(bf16[162,432]{1,0:T(8,128)(2,1)} %constant.34.clone.select_out) | copy-start | bytes 419908
  28.8 0.8 %copy-start.6 = (bf16[81,240]{1,0:T(8,128)(2,1)S(1)}, bf16[81,240]{1,0:T(8,128)(2,1)}, u32[]{:S(2)}) copy-start(bf16[81,240]{1,0:T(8,128)(2,1)} %constant.33.clone.select_in) | copy-start | bytes 116644
  30.0 0.7 copy-start.2
  30.7 0.6 copy-start.5
  31.3 0.6 copy-start.7
  34.4 16.0 %copy-start = (f32[288,128]{1,0:T(8,128)}, f32[288,128]{1,0:T(8,128)S(1)}, u32[]{:S(2)}) copy-start(f32[288,128]{1,0:T(8,128)S(1)} %shard_map.164.own) | copy-start | bytes 442372
  39.0 31.3 %all-to-all-start.1 = ((f32[256,1,384]{2,1,0:T(1,128)}), f32[256,1,384]{2,1,0:T(1,128)}, u32[]{:S(2)}, u32[]{:S(2)}) async-start(f32[256,1,384]{2,1,0:T(1,128)} %bitcast.17), calls=%async_computation.1 | async-start | bytes 786432 | tf_op jit(solution)/shard_map/all_to_all | solution.py:503
  50.4 14.6 %collective-permute-start.2 = (f32[216,128]{1,0:T(8,128)S(1)}, f32[216,128]{1,0:T(8,128)S(1)}, u32[]{:S(2)}, u32[]{:S(2)}) collective-permute-start(f32[216,128]{1,0:T(8,128)S(1)} %bitcast.20), channel_id=1, source_target_pairs={{0,1},{1,2},{2,3},{3,4},{4,5},{5,6},{6,7},{7,8},{8,9},{9,10},{10,1... | collective-permute-start | bytes 331784 | tf_op jit(solution)/shard_map/ppermute | solution.py:505
  50.6 14.4 %collective-permute-start.3 = (f32[216,128]{1,0:T(8,128)S(1)}, f32[216,128]{1,0:T(8,128)S(1)}, u32[]{:S(2)}, u32[]{:S(2)}) collective-permute-start(f32[216,128]{1,0:T(8,128)S(1)} %bitcast.19), channel_id=1, source_target_pairs={{1,0},{2,1},{3,2},{4,3},{5,4},{6,5},{7,6},{8,7},{9,8},{10,9},{11,1... | collective-permute-start | bytes 331784 | tf_op jit(solution)/shard_map/ppermute | solution.py:506
  65.0 0.6 copy-start.8
  65.6 0.7 copy-start.9

commit v2 on v1

--- a/solution.py
+++ b/solution.py
@@ -17,8 +17,7 @@
 spacing = 2.0 * math.pi / N
 bf16 = jnp.bfloat16
 f32 = jnp.float32
-FULL = 60 * 2**20
-MOST = 2**26 - 9 * 2**15
+MOST = 2**26 - 2**14
 PRE = 80
 STR = 144
 
@@ -135,23 +134,31 @@
     return one(left[0], right[0]) + (one(left[1], right[0]) + one(left[0], right[1]))
 
 
-def fetch(pairs, sems):
-    copies = [pltpu.make_async_copy(a, b, sems.at[i]) for i, (a, b) in enumerate(pairs)]
+def fetch(pairs, sems, at=0):
+    copies = [pltpu.make_async_copy(a, b, sems.at[at + i]) for i, (a, b) in enumerate(pairs)]
     for copy in copies:
         copy.start()
     return copies
 
 
-def transform_z(source_far, table_far, out, source, table, sems):
-    for copy in fetch([(source_far, source), (table_far, table)], sems):
-        copy.wait()
+def transform_z(source_far, table_far, velocity, out, last, first, source, table, sems):
+    pairs = [(source_far, source), (table_far, table)]
+    for c in range(3):
+        rows = pl.ds(c * 12, 12)
+        pairs.append((velocity.at[pl.ds(c * 64 + 52, 12), :], last.at[rows, :]))
+        pairs.append((velocity.at[pl.ds(c * 64, 12), :], first.at[rows, :]))
+    copies = fetch(pairs, sems)
+    copies[0].wait()
+    copies[1].wait()
     blocks = [[source[pl.ds(c * 64 + y, 16, stride=4), :] for y in range(4)] for c in range(3)]
-    first = jnp.concatenate(blocks[0] + blocks[1], 0)
-    second = jnp.concatenate(blocks[2] + blocks[2], 0)
-    for tile, cells in enumerate((first, second)):
+    flat = jnp.concatenate(blocks[0] + blocks[1], 0)
+    upright = jnp.concatenate(blocks[2] + blocks[2], 0)
+    for tile, cells in enumerate((flat, upright)):
         modes = product((table[tile, 0], table[tile, 1]), split(cells), (1, 1))
         for copy in range(2):
             out[pl.ds(2 * copy + tile, 128, stride=4), :] = modes
+    for copy in copies[2:]:
+        copy.wait()
 
 
 def project(
@@ -183,15 +190,21 @@
             (row_forward_far, row_forward),
             (twiddle_far, twiddle),
             (lane_forward_far, lane_forward),
+        ],
+        sems,
+    )
+    first.wait()
+    copies[0].wait()
+    copies += fetch(
+        [
             (waves_far, waves),
             (lane_backward_far.at[part], lane_backward),
             (twiddle_back_far.at[part], twiddle_back),
             (row_backward_far, row_backward),
         ],
         sems,
-    )
-    first.wait()
-    copies[0].wait()
+        4,
+    )
     tiles = [source[pl.ds(tile, 256, stride=2), :] for tile in range(2)]
     mixed = product((row_forward[0], row_forward[1]), split(jnp.concatenate(tiles, 1)))
     copies[1].wait()
@@ -231,53 +244,108 @@
         out[pl.ds(component, 256, stride=3), :] = block
 
 
-def extend_x(source, low, high, out):
-    for c in range(3):
-        for y in range(4):
-            base = (c * 4 + y) * 24
-            out[pl.ds(base + 16, 8), :] = jnp.zeros((8, 128), f32)
-            out[pl.ds(base, 16), :] = source[pl.ds(c * 64 + y, 16, stride=4), :]
-            out[pl.ds(base + 16, 3), :] = high[pl.ds(c * 12 + y, 3, stride=4), :]
-            out[pl.ds(base + 21, 3), :] = low[pl.ds(c * 12 + y, 3, stride=4), :]
-
-
-def sixth(at):
-    near, middle, far = [at(k) - at(-k) for k in (1, 2, 3)]
-    return (45.0 * near - 9.0 * middle + far) * (1.0 / (60.0 * spacing))
-
-
-def rolled(block, axis):
-    return lambda k: pltpu.roll(block, (-k) % block.shape[axis], axis)
-
-
-def band_weights(
+def arrange(
+    velocity_far,
+    low_far,
+    high_far,
+    kernel_in_far,
+    kernel_out_far,
+    bias_far,
+    select_in_far,
+    select_out_far,
+    select_back_far,
+    own,
+    last,
+    first,
+    bias_rows,
+    banded_in,
+    banded_out,
+    banded_back,
+    velocity,
+    low,
+    high,
     kernel_in,
     kernel_out,
+    bias,
     select_in,
     select_out,
     select_back,
-    banded_in,
-    banded_out,
-    banded_back,
+    lines_in,
+    lines_out,
+    sems,
 ):
+    far = [velocity_far, low_far, high_far, kernel_in_far, kernel_out_far, bias_far]
+    far += [select_in_far, select_out_far, select_back_far]
+    near = [velocity, low, high, kernel_in, kernel_out, bias, select_in, select_out, select_back]
+    for copy in fetch(list(zip(far, near)), sems):
+        copy.wait()
+    for c in range(3):
+        for y in range(4):
+            targets = [(own, (c * 4 + y) * 24)]
+            if y > 0:
+                targets.append((last, (c * 3 + y - 1) * 24))
+            if y < 3:
+                targets.append((first, (c * 3 + y) * 24))
+            for out, base in targets:
+                out[pl.ds(base + 16, 8), :] = jnp.zeros((8, 128), f32)
+                out[pl.ds(base, 16), :] = velocity[pl.ds(c * 64 + y, 16, stride=4), :]
+                out[pl.ds(base + 16, 3), :] = high[pl.ds(c * 12 + y, 3, stride=4), :]
+                out[pl.ds(base + 21, 3), :] = low[pl.ds(c * 12 + y, 3, stride=4), :]
+    square = (32, 32)
+    diagonal = lax.broadcasted_iota(jnp.int32, square, 0) == lax.broadcasted_iota(
+        jnp.int32, square, 1
+    )
+    column = jnp.sum(jnp.where(diagonal, jnp.broadcast_to(bias[...], square), 0.0), 1, keepdims=True)
+    column = jnp.broadcast_to(column, (32, 128))
+    for yo in range(6):
+        bias_rows[pl.ds(yo * 32, 32), :] = column
+    for kernel, lines, count in ((kernel_in, lines_in, 3), (kernel_out, lines_out, 6)):
+        for c in range(count):
+            for dx in range(3):
+                for dy in range(3):
+                    rows = pl.ds(((c * 3 + dx) * 3 + dy) * 3, 3)
+                    lines[rows, :] = kernel[c, dx, dy].astype(f32)
+    lines = lines_in[...].astype(bf16)
     over_rows = (((0,), (0,)), ((), ()))
     for kernel, select, banded in (
-        (kernel_in, select_in, banded_in),
-        (kernel_out, select_out, banded_out),
+        (lines, select_in, banded_in),
+        (lines_out[...].astype(bf16), select_out, banded_out),
     ):
-        band = lax.dot_general(kernel[...], select[...], over_rows, preferred_element_type=f32)
+        band = lax.dot_general(kernel, select[...], over_rows, preferred_element_type=f32)
         for yo in range(6):
             moved = band
             if yo:
                 moved = jnp.concatenate([jnp.zeros((32, yo), f32), band[:, :-yo]], 1)
             banded[pl.ds(yo * 32, 32), :] = moved.astype(bf16)
-    band = jnp.dot(select_back[...], kernel_in[...], preferred_element_type=f32).astype(bf16)
+    band = jnp.dot(select_back[...], lines, preferred_element_type=f32).astype(bf16)
     for block in range(18):
         banded_back[:, pl.ds(block * 32, 32)] = band[block * 48 : block * 48 + 48]
 
 
-def prepare(own, low, high, bias, banded_in, field, slope, slants, slabs, sems):
-    pairs = []
+def sixth(at):
+    near, middle, far = [at(k) - at(-k) for k in (1, 2, 3)]
+    return (45.0 * near - 9.0 * middle + far) * (1.0 / (60.0 * spacing))
+
+
+def rolled(block, axis):
+    return lambda k: pltpu.roll(block, (-k) % block.shape[axis], axis)
+
+
+def prepare(
+    own,
+    low,
+    high,
+    bias_far,
+    banded_in_far,
+    field,
+    slope,
+    slants,
+    slabs,
+    bias,
+    banded_in,
+    sems,
+):
+    pairs = [(bias_far, bias), (banded_in_far, banded_in)]
     for c in range(3):
         for source, start, rows in ((low, 0, 72), (own, 72, 96), (high, 168, 72)):
             target = field.at[pl.ds(c * 240 + start, rows), :]
@@ -285,6 +353,7 @@
     for copy in fetch(pairs, sems):
         copy.wait()
 
+    lift = jnp.concatenate([bias[...], bias[...]], 1)
     for i in range(20):
         row = (i + 22) % 24
         parts = [field[pl.ds(c * 240 + 24 + row, 8, stride=24), :] for c in range(3)]
@@ -296,7 +365,7 @@
                 slabs[pl.ds(j * PRE, PRE), pl.ds(half * 128, 128)] = slab
     for i in range(9):
         cells = slabs[pl.ds(i * PRE, 3 * PRE), :]
-        value = jnp.dot(banded_in[...], cells, preferred_element_type=f32) + bias[...]
+        value = jnp.dot(banded_in[...], cells, preferred_element_type=f32) + lift
         value = jnp.tanh(value)
         slope[pl.ds(i * 192, 192), :] = 1.0 - value * value
     for a in range(3):
@@ -422,7 +491,7 @@
             out[pl.ds(c * 64 + y, 16, stride=4), :] = block[:16] + time_step * total
 
 
-def call(kernel, shapes, args, spaces, scratch=(), copies=0, limit=24 * 2**20, flops=0):
+def call(kernel, shapes, args, spaces, outs, scratch=(), copies=0, limit=MOST, flops=0):
     size = 4 * sum(math.prod(s.shape) for s in shapes) + 4 * sum(math.prod(a.shape) for a in args)
     kinds = {"v": pltpu.VMEM, "s": pltpu.SMEM, "h": pltpu.HBM}
     scratch = list(scratch) + ([pltpu.SemaphoreType.DMA((copies,))] if copies else [])
@@ -430,7 +499,7 @@
         kernel,
         out_shape=shapes,
         in_specs=[pl.BlockSpec(memory_space=kinds[space]) for space in spaces],
-        out_specs=[pl.BlockSpec(memory_space=pltpu.VMEM)] * len(shapes),
+        out_specs=[pl.BlockSpec(memory_space=kinds[space]) for space in outs],
         scratch_shapes=scratch,
         compiler_params=pltpu.CompilerParams(vmem_limit_bytes=limit),
         cost_estimate=pl.CostEstimate(flops=flops, bytes_accessed=size, transcendentals=0),
@@ -443,18 +512,15 @@
 
 def body(velocity, cotangent, weight_in, bias_in, weight_out):
     t = {name: jnp.asarray(value) for name, value in constants().items()}
-    (modes,) = call(
+    modes, last, first = call(
         transform_z,
-        [shape(512)],
-        [cotangent.reshape(192, 128), t["forward_z"]],
-        "hh",
+        [shape(512), shape(36), shape(36)],
+        [cotangent.reshape(192, 128), t["forward_z"], velocity.reshape(192, 128)],
+        "hhh",
+        "vvv",
         [pltpu.VMEM((192, 128), f32), pltpu.VMEM((2, 2, 128, 128), bf16)],
-        2,
-        limit=FULL,
+        8,
         flops=4 * 2**22,
-    )
-    modes, velocity, weight_in, bias_in, weight_out = lax.optimization_barrier(
-        (modes, velocity, weight_in, bias_in, weight_out)
     )
     planes = lax.all_to_all(modes.reshape(256, 256), ("px", "py"), 0, 0, tiled=True)
     planes = planes.reshape(512, 128)
@@ -463,21 +529,31 @@
     down_x = [(b, a) for a, b in up_x]
     up_y = [(i, (i + 1) % PY) for i in range(PY)]
     down_y = [(b, a) for a, b in up_y]
-    low = lax.ppermute(velocity[:, 13:].reshape(36, 128), "px", up_x)
-    high = lax.ppermute(velocity[:, :3].reshape(36, 128), "px", down_x)
-    (own,) = call(extend_x, [shape(288)], [velocity.reshape(192, 128), low, high], "vvv")
-    kernel_in = weight_in.reshape(32, 81).T
-    kernel_out = weight_out.transpose(0, 2, 3, 4, 1).reshape(162, 32)
-    banded_in, banded_out, banded_back = call(
-        band_weights,
-        [shape(192, 3 * PRE, bf16), shape(192, 3 * STR, bf16), shape(48, 576, bf16)],
-        [kernel_in, kernel_out, t["select_in"], t["select_out"], t["select_back"]],
-        "vvvvv",
+    low = lax.ppermute(last, "px", up_x)
+    high = lax.ppermute(first, "px", down_x)
+    planes, low, high = lax.optimization_barrier((planes, low, high))
+    operands = [
+        velocity.reshape(192, 128),
+        low,
+        high,
+        weight_in.transpose(1, 2, 3, 4, 0),
+        weight_out.transpose(0, 2, 3, 4, 1),
+        bias_in.reshape(1, 32),
+        t["select_in"],
+        t["select_out"],
+        t["select_back"],
+    ]
+    own, last, first, bias, banded_in, banded_out, banded_back = call(
+        arrange,
+        [shape(288), shape(216), shape(216), shape(192)]
+        + [shape(192, 3 * PRE, bf16), shape(192, 3 * STR, bf16), shape(48, 576, bf16)],
+        operands,
+        "h" * 9,
+        "v" * 7,
+        [pltpu.VMEM(a.shape, a.dtype) for a in operands]
+        + [pltpu.VMEM((81, 32), f32), pltpu.VMEM((162, 32), f32)],
+        9,
         flops=2**27,
-    )
-    bias = jnp.tile(bias_in, 6).reshape(192, 1)
-    planes, own, bias, banded_in, banded_out, banded_back = lax.optimization_barrier(
-        (planes, own, bias, banded_in, banded_out, banded_back)
     )
     tables = [
         t["row_forward"],
@@ -494,24 +570,27 @@
         [shape(768)],
         [planes] + tables,
         "h" * 8,
+        "v",
         [pltpu.VMEM((512, 128), f32)]
         + [pltpu.VMEM(a.shape[picked.get(i, 0) :], a.dtype) for i, a in enumerate(tables)],
         8,
-        limit=MOST,
         flops=30 * 2 * 256**3,
     )
     received = lax.all_to_all(returned.reshape(256, 384), ("px", "py"), 0, 0, tiled=True)
-    layers = own.reshape(3, 96, 128)
-    low = lax.ppermute(layers[:, 24:].reshape(216, 128), "py", up_y)
-    high = lax.ppermute(layers[:, :72].reshape(216, 128), "py", down_y)
+    low = lax.ppermute(last, "py", up_y)
+    high = lax.ppermute(first, "py", down_y)
     field, slope, slants = call(
         prepare,
         [shape(720), shape(9 * 192, 256), shape(576)],
         [own, low, high, bias, banded_in],
-        "hhhvv",
-        [pltpu.VMEM((11 * PRE, 256), bf16)],
-        9,
-        limit=FULL,
+        "h" * 5,
+        "vvv",
+        [
+            pltpu.VMEM((11 * PRE, 256), bf16),
+            pltpu.VMEM((192, 128), f32),
+            pltpu.VMEM((192, 3 * PRE), bf16),
+        ],
+        11,
         flops=18 * 2 * 192 * 256 * 128,
     )
     operands = [
@@ -528,6 +607,7 @@
         [shape(192)],
         operands,
         "h" * 7,
+        "v",
         [pltpu.VMEM(a.shape, a.dtype) for a in operands]
         + [
             pltpu.VMEM((720, 128), f32),
@@ -537,7 +617,6 @@
             pltpu.VMEM((256, 128), f32),
         ],
         7,
-        limit=MOST,
         flops=2**29,
     )
     return result.reshape(3, 16, 4, 128)

time: 75.1 us -> 70.5 us (0.939)
  local copies, waits for them, and re-layouts: 9.76 us -> 0 us
  waiting for transfers between devices: 10.1 us -> 16 us
  starting transfers between devices: 39.4 us -> 37.2 us
  Pallas kernels: 14.9 us -> 16 us
    unnamed x20 -> x0, local copies, waits for them, and re-layouts: 5.84 us -> none
    ppermute x4, waiting for transfers between devices: 10.1 us -> 15.9 us  [the longest x1 8.42 us: body(): high = lax.ppermute(first, 'px', down_x)]
    all_to_all x1, starting transfers between devices: 11.4 us -> 9.28 us  [body(): lax.all_to_all(returned.reshape(256, 384), ('px', 'py'), 0, 0, tiled=True)]
    reshape x4 -> x0, local copies, waits for them, and re-layouts: 1.65 us -> none  [the longest x1 0.85 us: body(): kernel_out = weight_out.transpose(0, 2, 3, 4, 1).reshape(162, 32)]
    pallas_call x6 -> x5, Pallas kernels: 14.9 us -> 16 us  [call(): pl.pallas_call(kernel, out_shape=shapes, in_specs=[pl.BlockSpec(memory_sp...]
    optimization_barrier x1 -> x0, local copies, waits for them, and re-layouts: 0.77 us -> none  [body(): lax.optimization_barrier((planes, own, bias, banded_in, banded_out, bande...]
    slice x2 -> x0, local copies, waits for them, and re-layouts: 0.77 us -> none  [the longest x1 0.75 us: body(): high = lax.ppermute(velocity[:, :3].reshape(36, 128), 'px', down_x)]
  transfers between devices with their start and end apart: 6 -> 6, of which waited for: 2 -> 3; matrix products, arithmetic and copies ran while one was open for 5% -> 0% of each run, Pallas kernels for 6% -> 8%
where the time goes in v2:
time: 70.5 us; the launch traced here: 69.2 us
  starting transfers between devices  37.2 us (53%)
  Pallas kernels  16 us (23%)
  waiting for transfers between devices  16 us (23%)
    pallas_call x5, Pallas kernels, call(): pl.pallas_call(kernel, out_shape=shapes, in_specs=[pl.BlockSpec(memory_sp...  16 us
    all_to_all x1, starting transfers between devices, body(): lax.all_to_all(modes.reshape(256, 256), ('px', 'py'), 0, 0, tiled=True)  15.4 us
    all_to_all x1, starting transfers between devices, body(): lax.all_to_all(returned.reshape(256, 384), ('px', 'py'), 0, 0, tiled=True)  9.28 us
    ppermute x1, waiting for transfers between devices, body(): high = lax.ppermute(first, 'px', down_x)  8.42 us
    ppermute x1, starting transfers between devices, body(): low = lax.ppermute(last, 'px', up_x)  6.32 us
    ppermute x1, starting transfers between devices, body(): high = lax.ppermute(first, 'py', down_y)  5.92 us
    ppermute x1, waiting for transfers between devices, body(): low = lax.ppermute(last, 'py', up_y)  5.83 us
    ppermute x1, waiting for transfers between devices, body(): low = lax.ppermute(last, 'px', up_x)  1.69 us
  transfers between devices with their start and end apart: 6, of which 3 were waited for; matrix products, arithmetic and copies ran while one was open for 0% of the time, Pallas kernels for 8%

profile of v2, /device:TPU:24, one launch (start us, length us, event | category | flops | bytes accessed | tf_op | source)
XLA Modules:
  0.0 69.2 jit_solution(9667585815047611245)
XLA Ops:
  0.0 2.0 %shard_map.163 = (f32[512,128]{1,0:T(8,128)}, f32[36,128]{1,0:T(8,128)}, f32[36,128]{1,0:T(8,128)}) custom-call(f32[192,128]{1,0:T(8,128)} %bitcast.14, bf16[2,2,128,128]{3,2,1,0:T(8,128)(2,1)} %constant.24.clone.table_far, f32[192,128]{1,0:T(8,128)} %bitcast.11), custom_call_target="tpu_custom_call" | custom-call | flops 16777216 | bytes 757760 | tf_op jit(solution)/shard_map/pallas_call | solution.py:498
  2.0 15.4 %all-to-all-start = ((f32[256,1,256]{2,1,0:T(1,128)}), f32[256,1,256]{2,1,0:T(1,128)}, u32[]{:S(2)}, u32[]{:S(2)}) async-start(f32[256,1,256]{2,1,0:T(1,128)} %bitcast.13), calls=%async_computation | async-start | bytes 524288 | tf_op jit(solution)/shard_map/all_to_all | solution.py:525
  17.5 6.3 %collective-permute-start = (f32[36,128]{1,0:T(8,128)}, f32[36,128]{1,0:T(8,128)}, u32[]{:S(2)}, u32[]{:S(2)}) collective-permute-start(f32[36,128]{1,0:T(8,128)} %get-tuple-element.22), channel_id=1, source_target_pairs={{0,32},{32,64},{64,96},{96,128},{128,160},{160,192},{192,224},{224... | collective-permute-start | bytes 55304 | tf_op jit(solution)/shard_map/ppermute | solution.py:532
  23.8 0.0 collective-permute-start.1
  23.8 1.7 %collective-permute-done.low_far = f32[36,128]{1,0:T(8,128)} collective-permute-done((f32[36,128]{1,0:T(8,128)}, f32[36,128]{1,0:T(8,128)}, u32[]{:S(2)}, u32[]{:S(2)}) %collective-permute-start) | collective-permute-done | bytes 18464 | tf_op jit(solution)/shard_map/ppermute | solution.py:532
  25.5 8.4 %collective-permute-done.1.high_far = f32[36,128]{1,0:T(8,128)} collective-permute-done((f32[36,128]{1,0:T(8,128)}, f32[36,128]{1,0:T(8,128)}, u32[]{:S(2)}, u32[]{:S(2)}) %collective-permute-start.1) | collective-permute-done | bytes 18464 | tf_op jit(solution)/shard_map/ppermute | solution.py:533
  33.9 0.0 all-to-all-done
  33.9 4.5 %shard_map.164 = f32[768,128]{1,0:T(8,128)} custom-call(f32[512,128]{1,0:T(8,128)} %bitcast.3.source_far, bf16[2,512,256]{2,1,0:T(8,128)(2,1)} %constant.26.clone.row_forward_far, f32[2,256,128]{2,1,0:T(8,128)} %constant.28.clone.twiddle_far, bf16[2,256,256]{2,1,0:T(8,128)(2,1)} %constant.29.clone.lane_forward_far, f32[3,256,128]{2,1,0:T(8,128)} %constant.30.clone.waves_far, ...), custom_call_target="tpu_custom_call" | custom-call | flops 1006632960 | bytes 6553600 | tf_op jit(solution)/shard_map/pallas_call | solution.py:498
  38.4 9.3 %all-to-all-start.1 = ((f32[256,1,384]{2,1,0:T(1,128)}), f32[256,1,384]{2,1,0:T(1,128)}, u32[]{:S(2)}, u32[]{:S(2)}) async-start(f32[256,1,384]{2,1,0:T(1,128)} %bitcast.10), calls=%async_computation.1 | async-start | bytes 786432 | tf_op jit(solution)/shard_map/all_to_all | solution.py:579
  47.7 2.4 %shard_map.165 = (f32[288,128]{1,0:T(8,128)}, f32[216,128]{1,0:T(8,128)}, f32[216,128]{1,0:T(8,128)}, f32[192,128]{1,0:T(8,128)}, bf16[192,240]{1,0:T(8,128)(2,1...) custom-call(f32[192,128]{1,0:T(8,128)} %bitcast.12, f32[36,128]{1,0:T(8,128)} %collective-permute-done.low_far, ...), custom_call_target="tpu_custom_call" | custom-call | flops 134217728 | bytes 1897664 | tf_op jit(solution)/shard_map/pallas_call | solution.py:498
  50.1 0.2 collective-permute-start.2
  50.3 5.9 %collective-permute-start.3 = (f32[216,128]{1,0:T(8,128)}, f32[216,128]{1,0:T(8,128)}, u32[]{:S(2)}, u32[]{:S(2)}) collective-permute-start(f32[216,128]{1,0:T(8,128)} %get-tuple-element.29), channel_id=1, source_target_pairs={{1,0},{2,1},{3,2},{4,3},{5,4},{6,5},{7,6},{8,7},{9,8},{10,9},{11,1... | collective-permute-start | bytes 331784 | tf_op jit(solution)/shard_map/ppermute | solution.py:581
  56.3 5.8 %collective-permute-done.2.low = f32[216,128]{1,0:T(8,128)} collective-permute-done((f32[216,128]{1,0:T(8,128)}, f32[216,128]{1,0:T(8,128)}, u32[]{:S(2)}, u32[]{:S(2)}) %collective-permute-start.2) | collective-permute-done | bytes 110624 | tf_op jit(solution)/shard_map/ppermute | solution.py:580
  62.1 0.0 collective-permute-done.3.high
  62.1 3.0 %shard_map.166 = (f32[720,128]{1,0:T(8,128)}, f32[1728,256]{1,0:T(8,128)}, f32[576,128]{1,0:T(8,128)}) custom-call(f32[288,128]{1,0:T(8,128)} %get-tuple-element.27.own, f32[216,128]{1,0:T(8,128)} %collective-permute-done.2.low, f32[216,128]{1,0:T(8,128)} %collective-permute-done.3.high, f32[192,128]{1,0:T(8,128)} %get-tuple-element.30.bias_far, ...), custom_call_target="tpu_custom_call" | custom-call | flops 226492416 | bytes 3084288 | tf_op jit(solution)/shard_map/pallas_call | solution.py:498
  65.1 0.0 all-to-all-done.1
  65.2 4.1 %shard_map.167 = f32[192,128]{1,0:T(8,128)} custom-call(f32[768,128]{1,0:T(8,128)} %bitcast.5.modes_far, bf16[2,2,128,128]{3,2,1,0:T(8,128)(2,1)} %constant.25.clone.table_far, f32[720,128]{1,0:T(8,128)} %get-tuple-element.32.field_far, f32[576,128]{1,0:T(8,128)} %get-tuple-element.33.slants_far, f32[1728,256]{1,0:T(8,128)} %get-tuple-element.34.slope_far, ...), custom_call_target="tpu_custom_call" | custom-call | flops 536870912 | bytes 3629056 | tf_op jit(solution)/shard_map/pallas_call | solution.py:498
Async XLA Ops:
  2.0 31.9 %all-to-all-start = ((f32[256,1,256]{2,1,0:T(1,128)}), f32[256,1,256]{2,1,0:T(1,128)}, u32[]{:S(2)}, u32[]{:S(2)}) async-start(f32[256,1,256]{2,1,0:T(1,128)} %bitcast.13), calls=%async_computation | async-start | bytes 524288 | tf_op jit(solution)/shard_map/all_to_all | solution.py:525
  17.5 8.0 %collective-permute-start = (f32[36,128]{1,0:T(8,128)}, f32[36,128]{1,0:T(8,128)}, u32[]{:S(2)}, u32[]{:S(2)}) collective-permute-start(f32[36,128]{1,0:T(8,128)} %get-tuple-element.22), channel_id=1, source_target_pairs={{0,32},{32,64},{64,96},{96,128},{128,160},{160,192},{192,224},{224... | collective-permute-start | bytes 55304 | tf_op jit(solution)/shard_map/ppermute | solution.py:532
  23.8 10.1 %collective-permute-start.1 = (f32[36,128]{1,0:T(8,128)}, f32[36,128]{1,0:T(8,128)}, u32[]{:S(2)}, u32[]{:S(2)}) collective-permute-start(f32[36,128]{1,0:T(8,128)} %get-tuple-element.23), channel_id=1, source_target_pairs={{32,0},{64,32},{96,64},{128,96},{160,128},{192,160},{224,192},{0,2... | collective-permute-start | bytes 55304 | tf_op jit(solution)/shard_map/ppermute | solution.py:533
  38.4 26.8 %all-to-all-start.1 = ((f32[256,1,384]{2,1,0:T(1,128)}), f32[256,1,384]{2,1,0:T(1,128)}, u32[]{:S(2)}, u32[]{:S(2)}) async-start(f32[256,1,384]{2,1,0:T(1,128)} %bitcast.10), calls=%async_computation.1 | async-start | bytes 786432 | tf_op jit(solution)/shard_map/all_to_all | solution.py:579
  50.1 12.0 %collective-permute-start.2 = (f32[216,128]{1,0:T(8,128)}, f32[216,128]{1,0:T(8,128)}, u32[]{:S(2)}, u32[]{:S(2)}) collective-permute-start(f32[216,128]{1,0:T(8,128)} %get-tuple-element.28), channel_id=1, source_target_pairs={{0,1},{1,2},{2,3},{3,4},{4,5},{5,6},{6,7},{7,8},{8,9},{9,10},{10,1... | collective-permute-start | bytes 331784 | tf_op jit(solution)/shard_map/ppermute | solution.py:580
  50.3 11.8 %collective-permute-start.3 = (f32[216,128]{1,0:T(8,128)}, f32[216,128]{1,0:T(8,128)}, u32[]{:S(2)}, u32[]{:S(2)}) collective-permute-start(f32[216,128]{1,0:T(8,128)} %get-tuple-element.29), channel_id=1, source_target_pairs={{1,0},{2,1},{3,2},{4,3},{5,4},{6,5},{7,6},{8,7},{9,8},{10,9},{11,1... | collective-permute-start | bytes 331784 | tf_op jit(solution)/shard_map/ppermute | solution.py:581

commit v3 on v2

--- a/solution.py
+++ b/solution.py
@@ -30,7 +30,7 @@
 
 
 def complex_form(table):
-    return np.block([[table.real, table.imag], [-table.imag, table.real]])
+    return np.concatenate([table.real, table.imag], 1)
 
 
 @functools.cache
@@ -54,7 +54,6 @@
     phase = phase + b[None, :, None, None] * b[None, None, None, :] / PY
     rows = np.exp(-2j * np.pi * phase.reshape(256, 256))
     row_forward = halves(np.concatenate([rows.real, rows.imag], 0))
-    row_backward = halves(np.concatenate([rows.real, rows.imag], 1))
     phase = a[:, None, None, None] * x16 + b[None, :, None, None] * y4[:, None]
     twiddle = np.exp(-2j * np.pi * phase.reshape(256, 64) / N)
     twiddle = np.tile(twiddle, (1, 2))
@@ -67,9 +66,7 @@
     )
     m, l = m.reshape(256, 64), l.reshape(256, 64)
     kx, ky = np.where(m > 64, m - N, m), np.where(l > 64, l - N, l)
-    square = np.tile(kx * kx + ky * ky, (1, 2))
-    retain = np.tile((m != 64) & (l != 64), (1, 2))
-    waves = np.stack([np.concatenate([kx, ky], 1), square, retain]).astype(np.float32)
+    waves = np.concatenate([kx, ky], 1).astype(np.float32)
     r = np.arange(24)
     xe = np.where(r < 19, r, r - 24)
     lane_backward, twiddle_back = [], []
@@ -83,7 +80,7 @@
         phase = a[:, None, None, None] * xe + b[None, :, None, None] * ye[:, None]
         table = np.pad(np.exp(2j * np.pi * phase.reshape(256, 120) / N), ((0, 0), (0, 8)))
         twiddle_back.append(np.stack([table.real, table.imag]))
-    lane_backward = np.stack(lane_backward).reshape(2, 2, 2, 256, 256)
+    lane_backward = np.stack(lane_backward).reshape(2, 2, 2, 128, 256)
     twiddle_back = np.stack(twiddle_back).astype(np.float32)
     select_in = np.zeros((3, 3, 3, 3, 3 * PRE))
     select_out = np.zeros((6, 3, 3, 3, 3 * STR))
@@ -108,7 +105,6 @@
         forward_z=forward_z,
         backward_z=backward_z,
         row_forward=row_forward,
-        row_backward=row_backward,
         twiddle=twiddle,
         lane_forward=lane_forward,
         waves=waves,
@@ -126,12 +122,19 @@
 
 
 def product(left, right, over=(1, 0)):
+    left = jnp.concatenate([left[0], left[1], left[0]], over[0])
+    right = jnp.concatenate([right[0], right[0], right[1]], over[1])
     dims = (((over[0],), (over[1],)), ((), ()))
-
-    def one(a, b):
-        return lax.dot_general(a, b, dims, preferred_element_type=f32)
-
-    return one(left[0], right[0]) + (one(left[1], right[0]) + one(left[0], right[1]))
+    return lax.dot_general(left, right, dims, preferred_element_type=f32)
+
+
+def turner(tables):
+    whole = []
+    for half in range(2):
+        top = tables[half]
+        bottom = jnp.concatenate([-top[:, 128:], top[:, :128]], 1)
+        whole.append(jnp.concatenate([top, bottom], 0))
+    return whole
 
 
 def fetch(pairs, sems, at=0):
@@ -141,13 +144,17 @@
     return copies
 
 
-def transform_z(source_far, table_far, velocity, out, last, first, source, table, sems):
-    pairs = [(source_far, source), (table_far, table)]
-    for c in range(3):
-        rows = pl.ds(c * 12, 12)
-        pairs.append((velocity.at[pl.ds(c * 64 + 52, 12), :], last.at[rows, :]))
-        pairs.append((velocity.at[pl.ds(c * 64, 12), :], first.at[rows, :]))
-    copies = fetch(pairs, sems)
+def transform_z(source_far, table_far, velocity, out, even, odd, source, table, sems):
+    parity = lax.rem(lax.axis_index("px"), 2)
+    copies = fetch(
+        [
+            (source_far, source),
+            (table_far, table),
+            (velocity.at[:, pl.ds(13 * (1 - parity), 3)], even),
+            (velocity.at[:, pl.ds(13 * parity, 3)], odd),
+        ],
+        sems,
+    )
     copies[0].wait()
     copies[1].wait()
     blocks = [[source[pl.ds(c * 64 + y, 16, stride=4), :] for y in range(4)] for c in range(3)]
@@ -169,7 +176,6 @@
     waves_far,
     lane_backward_far,
     twiddle_back_far,
-    row_backward_far,
     out,
     source,
     row_forward,
@@ -178,7 +184,6 @@
     waves,
     lane_backward,
     twiddle_back,
-    row_backward,
     sems,
 ):
     device = lax.axis_index("px") * PY + lax.axis_index("py")
@@ -190,21 +195,14 @@
             (row_forward_far, row_forward),
             (twiddle_far, twiddle),
             (lane_forward_far, lane_forward),
-        ],
-        sems,
-    )
-    first.wait()
-    copies[0].wait()
-    copies += fetch(
-        [
             (waves_far, waves),
             (lane_backward_far.at[part], lane_backward),
             (twiddle_back_far.at[part], twiddle_back),
-            (row_backward_far, row_backward),
         ],
         sems,
-        4,
-    )
+    )
+    first.wait()
+    copies[0].wait()
     tiles = [source[pl.ds(tile, 256, stride=2), :] for tile in range(2)]
     mixed = product((row_forward[0], row_forward[1]), split(jnp.concatenate(tiles, 1)))
     copies[1].wait()
@@ -215,9 +213,13 @@
         real = mixed[:256, tile * 128 : tile * 128 + 128]
         imag = mixed[256:, tile * 128 : tile * 128 + 128]
         turned = jnp.concatenate([real * cos - imag * sin, real * sin + imag * cos], 1)
-        spectrum.append(product(split(turned), (lane_forward[0], lane_forward[1])))
+        spectrum.append(product(split(turned), turner(lane_forward)))
     copies[3].wait()
-    wave, square, retain = waves[0], waves[1], waves[2]
+    wave = waves[...]
+    square = wave * wave
+    square = square + pltpu.roll(square, 64, 1)
+    kept = jnp.where(wave == 64.0, 0.0, 1.0)
+    retain = kept * pltpu.roll(kept, 64, 1)
     inverse = 1.0 / jnp.maximum(square + kz * kz, 1.0)
     (hr, hi), (vr, vi) = [(s[:, :128], s[:, 128:]) for s in spectrum]
     flat_r, flat_i = hr * wave, hi * wave
@@ -234,11 +236,11 @@
     parts = []
     for component in range(3):
         matrix = lane_backward.at[component % 2]
-        cells = product(upright if component == 2 else flat, (matrix[0], matrix[1]))
+        cells = product(upright if component == 2 else flat, turner(matrix))
         real, imag = cells[:, :128], cells[:, 128:]
         parts.append(jnp.concatenate([real * cos - imag * sin, real * sin + imag * cos], 0))
-    copies[6].wait()
-    result = product((row_backward[0], row_backward[1]), split(jnp.concatenate(parts, 1)))
+    unrow = [jnp.concatenate([row_forward[h, :256], row_forward[h, 256:]], 1) for h in range(2)]
+    result = product(unrow, split(jnp.concatenate(parts, 1)))
     for component in range(3):
         block = result[:, component * 128 : component * 128 + 128]
         out[pl.ds(component, 256, stride=3), :] = block
@@ -246,8 +248,8 @@
 
 def arrange(
     velocity_far,
-    low_far,
-    high_far,
+    even_far,
+    odd_far,
     kernel_in_far,
     kernel_out_far,
     bias_far,
@@ -255,15 +257,14 @@
     select_out_far,
     select_back_far,
     own,
-    last,
-    first,
+    even,
+    odd,
     bias_rows,
     banded_in,
     banded_out,
     banded_back,
     velocity,
-    low,
-    high,
+    halo,
     kernel_in,
     kernel_out,
     bias,
@@ -274,23 +275,25 @@
     lines_out,
     sems,
 ):
-    far = [velocity_far, low_far, high_far, kernel_in_far, kernel_out_far, bias_far]
+    parity = lax.rem(lax.axis_index("px"), 2)
+    far = [velocity_far, even_far, odd_far, kernel_in_far, kernel_out_far, bias_far]
     far += [select_in_far, select_out_far, select_back_far]
-    near = [velocity, low, high, kernel_in, kernel_out, bias, select_in, select_out, select_back]
+    near = [velocity, halo.at[1 - parity], halo.at[parity], kernel_in, kernel_out, bias]
+    near += [select_in, select_out, select_back]
     for copy in fetch(list(zip(far, near)), sems):
         copy.wait()
     for c in range(3):
         for y in range(4):
-            targets = [(own, (c * 4 + y) * 24)]
-            if y > 0:
-                targets.append((last, (c * 3 + y - 1) * 24))
-            if y < 3:
-                targets.append((first, (c * 3 + y) * 24))
-            for out, base in targets:
-                out[pl.ds(base + 16, 8), :] = jnp.zeros((8, 128), f32)
-                out[pl.ds(base, 16), :] = velocity[pl.ds(c * 64 + y, 16, stride=4), :]
-                out[pl.ds(base + 16, 3), :] = high[pl.ds(c * 12 + y, 3, stride=4), :]
-                out[pl.ds(base + 21, 3), :] = low[pl.ds(c * 12 + y, 3, stride=4), :]
+            base = (c * 4 + y) * 24
+            own[pl.ds(base + 16, 8), :] = jnp.zeros((8, 128), f32)
+            own[pl.ds(base, 16), :] = velocity[pl.ds(c * 64 + y, 16, stride=4), :]
+            own[pl.ds(base + 16, 3), :] = halo[1, c, :, y, :]
+            own[pl.ds(base + 21, 3), :] = halo[0, c, :, y, :]
+    parity = lax.rem(lax.axis_index("py"), 2)
+    for c in range(3):
+        for out, skip in ((even, 1 - parity), (odd, parity)):
+            rows = pl.ds(pl.multiple_of((c * 4 + skip) * 24, 8), 72)
+            out[pl.ds(c * 72, 72), :] = own[rows, :]
     square = (32, 32)
     diagonal = lax.broadcasted_iota(jnp.int32, square, 0) == lax.broadcasted_iota(
         jnp.int32, square, 1
@@ -333,8 +336,8 @@
 
 def prepare(
     own,
-    low,
-    high,
+    even,
+    odd,
     bias_far,
     banded_in_far,
     field,
@@ -346,10 +349,16 @@
     sems,
 ):
     pairs = [(bias_far, bias), (banded_in_far, banded_in)]
+    parity = lax.rem(lax.axis_index("py"), 2)
     for c in range(3):
-        for source, start, rows in ((low, 0, 72), (own, 72, 96), (high, 168, 72)):
-            target = field.at[pl.ds(c * 240 + start, rows), :]
-            pairs.append((source.at[pl.ds(c * rows, rows), :], target))
+        for source, start, rows in (
+            (even, 168 * (1 - parity), 72),
+            (own, 72, 96),
+            (odd, 168 * parity, 72),
+        ):
+            start = c * 240 + start
+            start = start if isinstance(start, int) else pl.multiple_of(start, 8)
+            pairs.append((source.at[pl.ds(c * rows, rows), :], field.at[pl.ds(start, rows), :]))
     for copy in fetch(pairs, sems):
         copy.wait()
 
@@ -409,11 +418,11 @@
         [
             (modes_far, modes),
             (table_far, table),
+            (field_far, field),
+            (slants_far, slants),
             (banded_out_far, banded_out),
             (slope_far, slope),
             (banded_back_far, banded_back),
-            (field_far, field),
-            (slants_far, slants),
         ],
         sems,
     )
@@ -453,24 +462,6 @@
                 slabs[pl.ds(j * STR, STR), pl.ds(half * 128, 128)] = slab
     copies[2].wait()
     copies[3].wait()
-    for i in range(9):
-        cells = slabs[pl.ds(i * STR, 3 * STR), :]
-        value = jnp.dot(banded_out[...], cells, preferred_element_type=f32)
-        value = (value * slope[pl.ds(i * 192, 192), :]).astype(bf16)
-        for x, block in ((i, value[:, :128]), (i + 9, value[:, 128:])):
-            for half, j in enumerate((x, x - 8)):
-                if 0 <= j <= 9:
-                    adjoint[pl.ds(j * 192, 192), pl.ds(half * 128, 128)] = block
-    copies[4].wait()
-    for i in range(8):
-        cells = adjoint[pl.ds(i * 192, 576), :]
-        value = jnp.dot(banded_back[...], cells, preferred_element_type=f32)
-        for half in range(2):
-            block = value[:, half * 128 : half * 128 + 128]
-            total = block[16:32] + pltpu.roll(block[:16], 127, 1) + pltpu.roll(block[32:], 1, 1)
-            closure[pl.ds((i + 8 * half) * 16, 16), :] = total
-    copies[5].wait()
-    copies[6].wait()
     for c in range(3):
         across = [
             lam[pl.ds(c * 240 + y * 24, 16), :] * field[pl.ds(240 + y * 24, 16), :]
@@ -487,8 +478,29 @@
                 for a in range(3)
             ]
             total = total - (crossed[0] + crossed[1] + crossed[2])
-            total = total + closure[pl.ds(c * 4 + y, 16, stride=16), :]
             out[pl.ds(c * 64 + y, 16, stride=4), :] = block[:16] + time_step * total
+    copies[4].wait()
+    copies[5].wait()
+    for i in range(9):
+        cells = slabs[pl.ds(i * STR, 3 * STR), :]
+        value = jnp.dot(banded_out[...], cells, preferred_element_type=f32)
+        value = (value * slope[pl.ds(i * 192, 192), :]).astype(bf16)
+        for x, block in ((i, value[:, :128]), (i + 9, value[:, 128:])):
+            for half, j in enumerate((x, x - 8)):
+                if 0 <= j <= 9:
+                    adjoint[pl.ds(j * 192, 192), pl.ds(half * 128, 128)] = block
+    copies[6].wait()
+    for i in range(8):
+        cells = adjoint[pl.ds(i * 192, 576), :]
+        value = jnp.dot(banded_back[...], cells, preferred_element_type=f32)
+        for half in range(2):
+            block = value[:, half * 128 : half * 128 + 128]
+            total = block[16:32] + pltpu.roll(block[:16], 127, 1) + pltpu.roll(block[32:], 1, 1)
+            closure[pl.ds((i + 8 * half) * 16, 16), :] = total
+    for c in range(3):
+        for y in range(4):
+            rows = pl.ds(c * 64 + y, 16, stride=4)
+            out[rows, :] = out[rows, :] + time_step * closure[pl.ds(c * 4 + y, 16, stride=16), :]
 
 
 def call(kernel, shapes, args, spaces, outs, scratch=(), copies=0, limit=MOST, flops=0):
@@ -512,30 +524,31 @@
 
 def body(velocity, cotangent, weight_in, bias_in, weight_out):
     t = {name: jnp.asarray(value) for name, value in constants().items()}
-    modes, last, first = call(
+    modes, even, odd = call(
         transform_z,
-        [shape(512), shape(36), shape(36)],
-        [cotangent.reshape(192, 128), t["forward_z"], velocity.reshape(192, 128)],
+        [shape(512)] + [jax.ShapeDtypeStruct((3, 3, 4, 128), f32)] * 2,
+        [cotangent.reshape(192, 128), t["forward_z"], velocity],
         "hhh",
         "vvv",
         [pltpu.VMEM((192, 128), f32), pltpu.VMEM((2, 2, 128, 128), bf16)],
-        8,
+        4,
         flops=4 * 2**22,
     )
     planes = lax.all_to_all(modes.reshape(256, 256), ("px", "py"), 0, 0, tiled=True)
     planes = planes.reshape(512, 128)
 
-    up_x = [(i, (i + 1) % PX) for i in range(PX)]
-    down_x = [(b, a) for a, b in up_x]
-    up_y = [(i, (i + 1) % PY) for i in range(PY)]
-    down_y = [(b, a) for a, b in up_y]
-    low = lax.ppermute(last, "px", up_x)
-    high = lax.ppermute(first, "px", down_x)
-    planes, low, high = lax.optimization_barrier((planes, low, high))
+    def links(count):
+        odd = [(i, (i + 1) % count if i % 2 else (i - 1) % count) for i in range(count)]
+        return [(i, i ^ 1) for i in range(count)], odd
+
+    even_links, odd_links = links(PX)
+    even = lax.ppermute(even, "px", even_links)
+    odd = lax.ppermute(odd, "px", odd_links)
+    planes, even, odd = lax.optimization_barrier((planes, even, odd))
     operands = [
         velocity.reshape(192, 128),
-        low,
-        high,
+        even,
+        odd,
         weight_in.transpose(1, 2, 3, 4, 0),
         weight_out.transpose(0, 2, 3, 4, 1),
         bias_in.reshape(1, 32),
@@ -543,14 +556,15 @@
         t["select_out"],
         t["select_back"],
     ]
-    own, last, first, bias, banded_in, banded_out, banded_back = call(
+    own, even, odd, bias, banded_in, banded_out, banded_back = call(
         arrange,
         [shape(288), shape(216), shape(216), shape(192)]
         + [shape(192, 3 * PRE, bf16), shape(192, 3 * STR, bf16), shape(48, 576, bf16)],
         operands,
         "h" * 9,
         "v" * 7,
-        [pltpu.VMEM(a.shape, a.dtype) for a in operands]
+        [pltpu.VMEM((192, 128), f32), pltpu.VMEM((2, 3, 3, 4, 128), f32)]
+        + [pltpu.VMEM(a.shape, a.dtype) for a in operands[3:]]
         + [pltpu.VMEM((81, 32), f32), pltpu.VMEM((162, 32), f32)],
         9,
         flops=2**27,
@@ -562,27 +576,27 @@
         t["waves"],
         t["lane_backward"],
         t["twiddle_back"],
-        t["row_backward"],
     ]
     picked = {4: 1, 5: 1}
     (returned,) = call(
         project,
         [shape(768)],
         [planes] + tables,
-        "h" * 8,
+        "h" * 7,
         "v",
         [pltpu.VMEM((512, 128), f32)]
         + [pltpu.VMEM(a.shape[picked.get(i, 0) :], a.dtype) for i, a in enumerate(tables)],
-        8,
+        7,
         flops=30 * 2 * 256**3,
     )
     received = lax.all_to_all(returned.reshape(256, 384), ("px", "py"), 0, 0, tiled=True)
-    low = lax.ppermute(last, "py", up_y)
-    high = lax.ppermute(first, "py", down_y)
+    even_links, odd_links = links(PY)
+    even = lax.ppermute(even, "py", even_links)
+    odd = lax.ppermute(odd, "py", odd_links)
     field, slope, slants = call(
         prepare,
         [shape(720), shape(9 * 192, 256), shape(576)],
-        [own, low, high, bias, banded_in],
+        [own, even, odd, bias, banded_in],
         "h" * 5,
         "vvv",
         [

time: 70.5 us -> 69.9 us (level)
  starting transfers between devices: 37.2 us -> 41.9 us
  waiting for transfers between devices: 16 us -> 11.5 us
    ppermute x4, waiting for transfers between devices: 15.9 us -> 9.4 us  [the longest x1 6.22 us: body(): odd = lax.ppermute(odd, 'py', odd_links)]
    all_to_all x1, starting transfers between devices: 9.28 us -> 12.2 us  [body(): lax.all_to_all(returned.reshape(256, 384), ('px', 'py'), 0, 0, tiled=True)]
    all_to_all x1, waiting for transfers between devices: 0.01 us -> 2.09 us  [body(): lax.all_to_all(modes.reshape(256, 256), ('px', 'py'), 0, 0, tiled=True)]
    ppermute x4, starting transfers between devices: 12.5 us -> 14.3 us  [the longest x1 6.97 us: body(): odd = lax.ppermute(odd, 'px', odd_links)]
where the time goes in v3:
time: 69.9 us; the launch traced here: 69.3 us
  starting transfers between devices  41.9 us (60%)
  Pallas kernels  15.8 us (23%)
  waiting for transfers between devices  11.5 us (16%)
    pallas_call x5, Pallas kernels, call(): pl.pallas_call(kernel, out_shape=shapes, in_specs=[pl.BlockSpec(memory_sp...  15.8 us
    all_to_all x1, starting transfers between devices, body(): lax.all_to_all(modes.reshape(256, 256), ('px', 'py'), 0, 0, tiled=True)  15.4 us
    all_to_all x1, starting transfers between devices, body(): lax.all_to_all(returned.reshape(256, 384), ('px', 'py'), 0, 0, tiled=True)  12.2 us
    ppermute x1, starting transfers between devices, body(): odd = lax.ppermute(odd, 'px', odd_links)  6.97 us
    ppermute x1, waiting for transfers between devices, body(): odd = lax.ppermute(odd, 'py', odd_links)  6.22 us
    ppermute x1, starting transfers between devices, body(): odd = lax.ppermute(odd, 'py', odd_links)  6.19 us
    ppermute x1, waiting for transfers between devices, body(): odd = lax.ppermute(odd, 'px', odd_links)  3.18 us
    all_to_all x1, waiting for transfers between devices, body(): lax.all_to_all(modes.reshape(256, 256), ('px', 'py'), 0, 0, tiled=True)  2.09 us
  transfers between devices with their start and end apart: 6, of which 3 were waited for; matrix products, arithmetic and copies ran while one was open for 0% of the time, Pallas kernels for 8%

profile of v3, /device:TPU:24, one launch (start us, length us, event | category | flops | bytes accessed | tf_op | source)
XLA Modules:
  0.0 69.3 jit_solution(5049121901025362371)
XLA Ops:
  0.0 1.9 %shard_map.154 = (f32[512,128]{1,0:T(8,128)}, f32[3,3,4,128]{3,2,1,0:T(4,128)}, f32[3,3,4,128]{3,2,1,0:T(4,128)}) custom-call(f32[192,128]{1,0:T(8,128)} %bitcast.13, bf16[2,2,128,128]{3,2,1,0:T(8,128)(2,1)} %constant.22.clone.table_far, f32[3,16,4,128]{3,2,1,0:T(4,128)} %velocity.1), custom_call_target="tpu_custom_call" | custom-call | flops 16777216 | bytes 757760 | tf_op jit(solution)/shard_map/pallas_call | solution.py:510
  1.9 15.4 %all-to-all-start = ((f32[256,1,256]{2,1,0:T(1,128)}), f32[256,1,256]{2,1,0:T(1,128)}, u32[]{:S(2)}, u32[]{:S(2)}) async-start(f32[256,1,256]{2,1,0:T(1,128)} %bitcast.12), calls=%async_computation | async-start | bytes 524288 | tf_op jit(solution)/shard_map/all_to_all | solution.py:537
  17.4 0.9 %collective-permute-start = (f32[3,3,4,128]{3,2,1,0:T(4,128)}, f32[3,3,4,128]{3,2,1,0:T(4,128)}, u32[]{:S(2)}, u32[]{:S(2)}) collective-permute-start(f32[3,3,4,128]{3,2,1,0:T(4,128)} %get-tuple-element.22), channel_id=1, source_target_pairs={{0,32},{32,0},{64,96},{96,64},{128,160},{160,128},{192,224},{224,1... | collective-permute-start | bytes 55304 | tf_op jit(solution)/shard_map/ppermute | solution.py:545
  18.3 7.0 %collective-permute-start.1 = (f32[3,3,4,128]{3,2,1,0:T(4,128)}, f32[3,3,4,128]{3,2,1,0:T(4,128)}, u32[]{:S(2)}, u32[]{:S(2)}) collective-permute-start(f32[3,3,4,128]{3,2,1,0:T(4,128)} %get-tuple-element.23), channel_id=1, source_target_pairs={{0,224},{32,64},{64,32},{96,128},{128,96},{160,192},{192,160},{224... | collective-permute-start | bytes 55304 | tf_op jit(solution)/shard_map/ppermute | solution.py:546
  25.2 0.0 collective-permute-done.even_far
  25.2 3.2 %collective-permute-done.1.odd_far = f32[3,3,4,128]{3,2,1,0:T(4,128)} collective-permute-done((f32[3,3,4,128]{3,2,1,0:T(4,128)}, f32[3,3,4,128]{3,2,1,0:T(4,128)}, u32[]{:S(2)}, u32[]{:S(2)}) %collective-permute-start.1) | collective-permute-done | bytes 18464 | tf_op jit(solution)/shard_map/ppermute | solution.py:546
  28.4 2.1 %all-to-all-done = f32[256,1,256]{2,1,0:T(1,128)} async-done(((f32[256,1,256]{2,1,0:T(1,128)}), f32[256,1,256]{2,1,0:T(1,128)}, u32[]{:S(2)}, u32[]{:S(2)}) %all-to-all-start) | async-done | bytes 262176 | tf_op jit(solution)/shard_map/all_to_all | solution.py:537
  30.5 4.3 %shard_map.155 = f32[768,128]{1,0:T(8,128)} custom-call(f32[512,128]{1,0:T(8,128)} %bitcast.2.source_far, bf16[2,512,256]{2,1,0:T(8,128)(2,1)} %constant.24.clone.row_forward_far, f32[2,256,128]{2,1,0:T(8,128)} %constant.25.clone.twiddle_far, bf16[2,128,256]{2,1,0:T(8,128)(2,1)} %constant.26.clone.lane_forward_far, f32[256,128]{1,0:T(8,128)} %constant.27.clone.waves_far, ...), custom_call_target="tpu_custom_call" | custom-call | flops 1006632960 | bytes 3932160 | tf_op jit(solution)/shard_map/pallas_call | solution.py:510
  34.9 12.2 %all-to-all-start.1 = ((f32[256,1,384]{2,1,0:T(1,128)}), f32[256,1,384]{2,1,0:T(1,128)}, u32[]{:S(2)}, u32[]{:S(2)}) async-start(f32[256,1,384]{2,1,0:T(1,128)} %bitcast.10), calls=%async_computation.1 | async-start | bytes 786432 | tf_op jit(solution)/shard_map/all_to_all | solution.py:592
  47.1 2.5 %shard_map.156 = (f32[288,128]{1,0:T(8,128)}, f32[216,128]{1,0:T(8,128)}, f32[216,128]{1,0:T(8,128)}, f32[192,128]{1,0:T(8,128)}, bf16[192,240]{1,0:T(8,128)(2,1...) custom-call(f32[192,128]{1,0:T(8,128)} %bitcast.11, f32[3,3,4,128]{3,2,1,0:T(4,128)} %collective-permute-done.even_far, ...), custom_call_target="tpu_custom_call" | custom-call | flops 134217728 | bytes 1897664 | tf_op jit(solution)/shard_map/pallas_call | solution.py:510
  49.6 0.2 collective-permute-start.2
  49.8 6.2 %collective-permute-start.3 = (f32[216,128]{1,0:T(8,128)}, f32[216,128]{1,0:T(8,128)}, u32[]{:S(2)}, u32[]{:S(2)}) collective-permute-start(f32[216,128]{1,0:T(8,128)} %get-tuple-element.29), channel_id=1, source_target_pairs={{0,31},{1,2},{2,1},{3,4},{4,3},{5,6},{6,5},{7,8},{8,7},{9,10},{10,... | collective-permute-start | bytes 331784 | tf_op jit(solution)/shard_map/ppermute | solution.py:595
  56.0 0.0 collective-permute-done.2.even
  56.0 6.2 %collective-permute-done.3.odd = f32[216,128]{1,0:T(8,128)} collective-permute-done((f32[216,128]{1,0:T(8,128)}, f32[216,128]{1,0:T(8,128)}, u32[]{:S(2)}, u32[]{:S(2)}) %collective-permute-start.3) | collective-permute-done | bytes 110624 | tf_op jit(solution)/shard_map/ppermute | solution.py:595
  62.2 3.0 %shard_map.157 = (f32[720,128]{1,0:T(8,128)}, f32[1728,256]{1,0:T(8,128)}, f32[576,128]{1,0:T(8,128)}) custom-call(f32[288,128]{1,0:T(8,128)} %get-tuple-element.27.own, f32[216,128]{1,0:T(8,128)} %collective-permute-done.2.even, f32[216,128]{1,0:T(8,128)} %collective-permute-done.3.odd, f32[192,128]{1,0:T(8,128)} %get-tuple-element.30.bias_far, ...), custom_call_target="tpu_custom_call" | custom-call | flops 226492416 | bytes 3084288 | tf_op jit(solution)/shard_map/pallas_call | solution.py:510
  65.3 0.0 all-to-all-done.1
  65.3 4.0 %shard_map.158 = f32[192,128]{1,0:T(8,128)} custom-call(f32[768,128]{1,0:T(8,128)} %bitcast.4.modes_far, bf16[2,2,128,128]{3,2,1,0:T(8,128)(2,1)} %constant.23.clone.table_far, f32[720,128]{1,0:T(8,128)} %get-tuple-element.32.field_far, f32[576,128]{1,0:T(8,128)} %get-tuple-element.33.slants_far, f32[1728,256]{1,0:T(8,128)} %get-tuple-element.34.slope_far, ...), custom_call_target="tpu_custom_call" | custom-call | flops 536870912 | bytes 3629056 | tf_op jit(solution)/shard_map/pallas_call | solution.py:510
Async XLA Ops:
  1.9 28.6 %all-to-all-start = ((f32[256,1,256]{2,1,0:T(1,128)}), f32[256,1,256]{2,1,0:T(1,128)}, u32[]{:S(2)}, u32[]{:S(2)}) async-start(f32[256,1,256]{2,1,0:T(1,128)} %bitcast.12), calls=%async_computation | async-start | bytes 524288 | tf_op jit(solution)/shard_map/all_to_all | solution.py:537
  17.4 7.9 %collective-permute-start = (f32[3,3,4,128]{3,2,1,0:T(4,128)}, f32[3,3,4,128]{3,2,1,0:T(4,128)}, u32[]{:S(2)}, u32[]{:S(2)}) collective-permute-start(f32[3,3,4,128]{3,2,1,0:T(4,128)} %get-tuple-element.22), channel_id=1, source_target_pairs={{0,32},{32,0},{64,96},{96,64},{128,160},{160,128},{192,224},{224,1... | collective-permute-start | bytes 55304 | tf_op jit(solution)/shard_map/ppermute | solution.py:545
  18.3 10.1 %collective-permute-start.1 = (f32[3,3,4,128]{3,2,1,0:T(4,128)}, f32[3,3,4,128]{3,2,1,0:T(4,128)}, u32[]{:S(2)}, u32[]{:S(2)}) collective-permute-start(f32[3,3,4,128]{3,2,1,0:T(4,128)} %get-tuple-element.23), channel_id=1, source_target_pairs={{0,224},{32,64},{64,32},{96,128},{128,96},{160,192},{192,160},{224... | collective-permute-start | bytes 55304 | tf_op jit(solution)/shard_map/ppermute | solution.py:546
  34.9 30.4 %all-to-all-start.1 = ((f32[256,1,384]{2,1,0:T(1,128)}), f32[256,1,384]{2,1,0:T(1,128)}, u32[]{:S(2)}, u32[]{:S(2)}) async-start(f32[256,1,384]{2,1,0:T(1,128)} %bitcast.10), calls=%async_computation.1 | async-start | bytes 786432 | tf_op jit(solution)/shard_map/all_to_all | solution.py:592
  49.6 6.4 %collective-permute-start.2 = (f32[216,128]{1,0:T(8,128)}, f32[216,128]{1,0:T(8,128)}, u32[]{:S(2)}, u32[]{:S(2)}) collective-permute-start(f32[216,128]{1,0:T(8,128)} %get-tuple-element.28), channel_id=1, source_target_pairs={{0,1},{1,0},{2,3},{3,2},{4,5},{5,4},{6,7},{7,6},{8,9},{9,8},{10,11... | collective-permute-start | bytes 331784 | tf_op jit(solution)/shard_map/ppermute | solution.py:594
  49.8 12.4 %collective-permute-start.3 = (f32[216,128]{1,0:T(8,128)}, f32[216,128]{1,0:T(8,128)}, u32[]{:S(2)}, u32[]{:S(2)}) collective-permute-start(f32[216,128]{1,0:T(8,128)} %get-tuple-element.29), channel_id=1, source_target_pairs={{0,31},{1,2},{2,1},{3,4},{4,3},{5,6},{6,5},{7,8},{8,7},{9,10},{10,... | collective-permute-start | bytes 331784 | tf_op jit(solution)/shard_map/ppermute | solution.py:595

commit v4 on v3

--- a/solution.py
+++ b/solution.py
@@ -104,10 +104,8 @@
     return dict(
         forward_z=forward_z,
         backward_z=backward_z,
-        row_forward=row_forward,
-        twiddle=twiddle,
-        lane_forward=lane_forward,
-        waves=waves,
+        mixing=np.concatenate([row_forward, lane_forward], 1),
+        turning=np.concatenate([twiddle, waves[None]], 0),
         lane_backward=lane_backward,
         twiddle_back=twiddle_back,
         select_in=select_in,
@@ -170,18 +168,14 @@
 
 def project(
     source_far,
-    row_forward_far,
-    twiddle_far,
-    lane_forward_far,
-    waves_far,
+    mixing_far,
+    turning_far,
     lane_backward_far,
     twiddle_back_far,
     out,
     source,
-    row_forward,
-    twiddle,
-    lane_forward,
-    waves,
+    mixing,
+    turning,
     lane_backward,
     twiddle_back,
     sems,
@@ -192,10 +186,8 @@
     first, *copies = fetch(
         [
             (source_far, source),
-            (row_forward_far, row_forward),
-            (twiddle_far, twiddle),
-            (lane_forward_far, lane_forward),
-            (waves_far, waves),
+            (mixing_far, mixing),
+            (turning_far, turning),
             (lane_backward_far.at[part], lane_backward),
             (twiddle_back_far.at[part], twiddle_back),
         ],
@@ -204,18 +196,16 @@
     first.wait()
     copies[0].wait()
     tiles = [source[pl.ds(tile, 256, stride=2), :] for tile in range(2)]
-    mixed = product((row_forward[0], row_forward[1]), split(jnp.concatenate(tiles, 1)))
+    mixed = product((mixing[0, :512], mixing[1, :512]), split(jnp.concatenate(tiles, 1)))
     copies[1].wait()
-    copies[2].wait()
-    cos, sin = twiddle[0], twiddle[1]
+    cos, sin = turning[0], turning[1]
     spectrum = []
     for tile in range(2):
         real = mixed[:256, tile * 128 : tile * 128 + 128]
         imag = mixed[256:, tile * 128 : tile * 128 + 128]
         turned = jnp.concatenate([real * cos - imag * sin, real * sin + imag * cos], 1)
-        spectrum.append(product(split(turned), turner(lane_forward)))
-    copies[3].wait()
-    wave = waves[...]
+        spectrum.append(product(split(turned), turner(mixing.at[:, pl.ds(512, 128)])))
+    wave = turning[2]
     square = wave * wave
     square = square + pltpu.roll(square, 64, 1)
     kept = jnp.where(wave == 64.0, 0.0, 1.0)
@@ -230,8 +220,8 @@
     flat = jnp.concatenate([(hr - wave * dot_r) * retain, (hi - wave * dot_i) * retain], 1)
     upright = jnp.concatenate([(vr + kz * dot_i) * retain, (vi - kz * dot_r) * retain], 1)
     flat, upright = split(flat), split(upright)
-    copies[4].wait()
-    copies[5].wait()
+    copies[2].wait()
+    copies[3].wait()
     cos, sin = twiddle_back[0], twiddle_back[1]
     parts = []
     for component in range(3):
@@ -239,48 +229,17 @@
         cells = product(upright if component == 2 else flat, turner(matrix))
         real, imag = cells[:, :128], cells[:, 128:]
         parts.append(jnp.concatenate([real * cos - imag * sin, real * sin + imag * cos], 0))
-    unrow = [jnp.concatenate([row_forward[h, :256], row_forward[h, 256:]], 1) for h in range(2)]
+    unrow = [jnp.concatenate([mixing[h, :256], mixing[h, 256:512]], 1) for h in range(2)]
     result = product(unrow, split(jnp.concatenate(parts, 1)))
     for component in range(3):
         block = result[:, component * 128 : component * 128 + 128]
         out[pl.ds(component, 256, stride=3), :] = block
 
 
-def arrange(
-    velocity_far,
-    even_far,
-    odd_far,
-    kernel_in_far,
-    kernel_out_far,
-    bias_far,
-    select_in_far,
-    select_out_far,
-    select_back_far,
-    own,
-    even,
-    odd,
-    bias_rows,
-    banded_in,
-    banded_out,
-    banded_back,
-    velocity,
-    halo,
-    kernel_in,
-    kernel_out,
-    bias,
-    select_in,
-    select_out,
-    select_back,
-    lines_in,
-    lines_out,
-    sems,
-):
+def arrange(velocity_far, even_far, odd_far, own, even, odd, velocity, halo, sems):
     parity = lax.rem(lax.axis_index("px"), 2)
-    far = [velocity_far, even_far, odd_far, kernel_in_far, kernel_out_far, bias_far]
-    far += [select_in_far, select_out_far, select_back_far]
-    near = [velocity, halo.at[1 - parity], halo.at[parity], kernel_in, kernel_out, bias]
-    near += [select_in, select_out, select_back]
-    for copy in fetch(list(zip(far, near)), sems):
+    near = [velocity, halo.at[1 - parity], halo.at[parity]]
+    for copy in fetch(list(zip([velocity_far, even_far, odd_far], near)), sems):
         copy.wait()
     for c in range(3):
         for y in range(4):
@@ -294,6 +253,33 @@
         for out, skip in ((even, 1 - parity), (odd, parity)):
             rows = pl.ds(pl.multiple_of((c * 4 + skip) * 24, 8), 72)
             out[pl.ds(c * 72, 72), :] = own[rows, :]
+
+
+def band_weights(
+    kernel_in_far,
+    kernel_out_far,
+    bias_far,
+    select_in_far,
+    select_out_far,
+    select_back_far,
+    bias_rows,
+    banded_in,
+    banded_out,
+    banded_back,
+    kernel_in,
+    kernel_out,
+    bias,
+    select_in,
+    select_out,
+    select_back,
+    lines_in,
+    lines_out,
+    sems,
+):
+    far = [kernel_in_far, kernel_out_far, bias_far, select_in_far, select_out_far, select_back_far]
+    near = [kernel_in, kernel_out, bias, select_in, select_out, select_back]
+    for copy in fetch(list(zip(far, near)), sems):
+        copy.wait()
     square = (32, 32)
     diagonal = lax.broadcasted_iota(jnp.int32, square, 0) == lax.broadcasted_iota(
         jnp.int32, square, 1
@@ -534,21 +520,12 @@
         4,
         flops=4 * 2**22,
     )
+    modes, weight_in, bias_in, weight_out = lax.optimization_barrier(
+        (modes, weight_in, bias_in, weight_out)
+    )
     planes = lax.all_to_all(modes.reshape(256, 256), ("px", "py"), 0, 0, tiled=True)
     planes = planes.reshape(512, 128)
-
-    def links(count):
-        odd = [(i, (i + 1) % count if i % 2 else (i - 1) % count) for i in range(count)]
-        return [(i, i ^ 1) for i in range(count)], odd
-
-    even_links, odd_links = links(PX)
-    even = lax.ppermute(even, "px", even_links)
-    odd = lax.ppermute(odd, "px", odd_links)
-    planes, even, odd = lax.optimization_barrier((planes, even, odd))
     operands = [
-        velocity.reshape(192, 128),
-        even,
-        odd,
         weight_in.transpose(1, 2, 3, 4, 0),
         weight_out.transpose(0, 2, 3, 4, 1),
         bias_in.reshape(1, 32),
@@ -556,37 +533,53 @@
         t["select_out"],
         t["select_back"],
     ]
-    own, even, odd, bias, banded_in, banded_out, banded_back = call(
+    bands = call(
+        band_weights,
+        [shape(192), shape(192, 3 * PRE, bf16), shape(192, 3 * STR, bf16), shape(48, 576, bf16)],
+        operands,
+        "h" * 6,
+        "v" * 4,
+        [pltpu.VMEM(a.shape, a.dtype) for a in operands]
+        + [pltpu.VMEM((81, 32), f32), pltpu.VMEM((162, 32), f32)],
+        6,
+        flops=2**27,
+    )
+
+    def links(count):
+        odd = [(i, (i + 1) % count if i % 2 else (i - 1) % count) for i in range(count)]
+        return [(i, i ^ 1) for i in range(count)], odd
+
+    even_links, odd_links = links(PX)
+    even = lax.ppermute(even, "px", even_links)
+    odd = lax.ppermute(odd, "px", odd_links)
+    planes, even, odd, bands = lax.optimization_barrier((planes, even, odd, bands))
+    bias, banded_in, banded_out, banded_back = bands
+    own, even, odd = call(
         arrange,
-        [shape(288), shape(216), shape(216), shape(192)]
-        + [shape(192, 3 * PRE, bf16), shape(192, 3 * STR, bf16), shape(48, 576, bf16)],
-        operands,
-        "h" * 9,
-        "v" * 7,
-        [pltpu.VMEM((192, 128), f32), pltpu.VMEM((2, 3, 3, 4, 128), f32)]
-        + [pltpu.VMEM(a.shape, a.dtype) for a in operands[3:]]
-        + [pltpu.VMEM((81, 32), f32), pltpu.VMEM((162, 32), f32)],
-        9,
-        flops=2**27,
+        [shape(288), shape(216), shape(216)],
+        [velocity.reshape(192, 128), even, odd],
+        "hhh",
+        "vvv",
+        [pltpu.VMEM((192, 128), f32), pltpu.VMEM((2, 3, 3, 4, 128), f32)],
+        3,
+        flops=2**24,
     )
     tables = [
-        t["row_forward"],
-        t["twiddle"],
-        t["lane_forward"],
-        t["waves"],
+        t["mixing"],
+        t["turning"],
         t["lane_backward"],
         t["twiddle_back"],
     ]
-    picked = {4: 1, 5: 1}
+    picked = {2: 1, 3: 1}
     (returned,) = call(
         project,
         [shape(768)],
         [planes] + tables,
-        "h" * 7,
+        "h" * 5,
         "v",
         [pltpu.VMEM((512, 128), f32)]
         + [pltpu.VMEM(a.shape[picked.get(i, 0) :], a.dtype) for i, a in enumerate(tables)],
-        7,
+        5,
         flops=30 * 2 * 256**3,
     )
     received = lax.all_to_all(returned.reshape(256, 384), ("px", "py"), 0, 0, tiled=True)

time: 69.9 us -> 69.7 us (level)
  waiting for transfers between devices: 11.5 us -> 9.61 us
  Pallas kernels: 15.8 us -> 17 us
    ppermute x1, waiting for transfers between devices: 3.18 us -> 0.96 us  [body(): odd = lax.ppermute(odd, 'px', odd_links)]
    pallas_call x5 -> x6, Pallas kernels: 15.8 us -> 17 us  [call(): pl.pallas_call(kernel, out_shape=shapes, in_specs=[pl.BlockSpec(memory_sp...]
  transfers between devices with their start and end apart: 6 -> 6, of which waited for: 3 -> 3; matrix products, arithmetic and copies ran while one was open for 0% -> 0% of each run, Pallas kernels for 8% -> 10%
where the time goes in v4:
time: 69.7 us; the launch traced here: 68.6 us
  starting transfers between devices  42 us (60%)
  Pallas kernels  17 us (24%)
  waiting for transfers between devices  9.61 us (14%)
    pallas_call x6, Pallas kernels, call(): pl.pallas_call(kernel, out_shape=shapes, in_specs=[pl.BlockSpec(memory_sp...  17 us
    all_to_all x1, starting transfers between devices, body(): lax.all_to_all(modes.reshape(256, 256), ('px', 'py'), 0, 0, tiled=True)  15.4 us
    all_to_all x1, starting transfers between devices, body(): lax.all_to_all(returned.reshape(256, 384), ('px', 'py'), 0, 0, tiled=True)  12.2 us
    ppermute x1, starting transfers between devices, body(): odd = lax.ppermute(odd, 'px', odd_links)  6.97 us
    ppermute x1, waiting for transfers between devices, body(): odd = lax.ppermute(odd, 'py', odd_links)  6.58 us
    ppermute x1, starting transfers between devices, body(): odd = lax.ppermute(odd, 'py', odd_links)  6.19 us
    all_to_all x1, waiting for transfers between devices, body(): lax.all_to_all(modes.reshape(256, 256), ('px', 'py'), 0, 0, tiled=True)  2.07 us
  transfers between devices with their start and end apart: 6, of which 3 were waited for; matrix products, arithmetic and copies ran while one was open for 0% of the time, Pallas kernels for 10%

profile of v4, /device:TPU:24, one launch (start us, length us, event | category | flops | bytes accessed | tf_op | source)
XLA Modules:
  0.0 68.6 jit_solution(3024604170871080588)
XLA Ops:
  0.0 1.9 %shard_map.136 = (f32[512,128]{1,0:T(8,128)}, f32[3,3,4,128]{3,2,1,0:T(4,128)}, f32[3,3,4,128]{3,2,1,0:T(4,128)}) custom-call(f32[192,128]{1,0:T(8,128)} %bitcast.13, bf16[2,2,128,128]{3,2,1,0:T(8,128)(2,1)} %constant.18.clone.table_far, f32[3,16,4,128]{3,2,1,0:T(4,128)} %velocity.1), custom_call_target="tpu_custom_call" | custom-call | flops 16777216 | bytes 757760 | tf_op jit(solution)/shard_map/pallas_call | solution.py:496
  1.9 15.4 %all-to-all-start = ((f32[256,1,256]{2,1,0:T(1,128)}), f32[256,1,256]{2,1,0:T(1,128)}, u32[]{:S(2)}, u32[]{:S(2)}) async-start(f32[256,1,256]{2,1,0:T(1,128)} %bitcast.12), calls=%async_computation | async-start | bytes 524288 | tf_op jit(solution)/shard_map/all_to_all | solution.py:526
  17.4 0.9 %collective-permute-start = (f32[3,3,4,128]{3,2,1,0:T(4,128)}, f32[3,3,4,128]{3,2,1,0:T(4,128)}, u32[]{:S(2)}, u32[]{:S(2)}) collective-permute-start(f32[3,3,4,128]{3,2,1,0:T(4,128)} %get-tuple-element.31), channel_id=1, source_target_pairs={{0,32},{32,0},{64,96},{96,64},{128,160},{160,128},{192,224},{224,1... | collective-permute-start | bytes 55304 | tf_op jit(solution)/shard_map/ppermute | solution.py:553
  18.3 7.0 %collective-permute-start.1 = (f32[3,3,4,128]{3,2,1,0:T(4,128)}, f32[3,3,4,128]{3,2,1,0:T(4,128)}, u32[]{:S(2)}, u32[]{:S(2)}) collective-permute-start(f32[3,3,4,128]{3,2,1,0:T(4,128)} %get-tuple-element.32), channel_id=1, source_target_pairs={{0,224},{32,64},{64,32},{96,128},{128,96},{160,192},{192,160},{224... | collective-permute-start | bytes 55304 | tf_op jit(solution)/shard_map/ppermute | solution.py:554
  25.2 2.2 %shard_map.137 = (f32[192,128]{1,0:T(8,128)}, bf16[192,240]{1,0:T(8,128)(2,1)}, bf16[192,432]{1,0:T(8,128)(2,1)}, bf16[48,576]{1,0:T(8,128)(2,1)}) custom-call(bf16[3,3,3,3,32]{4,3,2,1,0:T(4,128)(2,1)} %bitcast.15, bf16[6,3,3,3,32]{4,3,2,1,0:T(4,128)(2,1)} %bitcast.14, f32[1,32]{1,0:T(1,128)} %bitcast.16, bf16[81,240]{1,0:T(8,128)(2,1)} %constant.24.clone.select_in_far, ...), custom_call_target="tpu_custom_call" | custom-call | flops 134217728 | bytes 1393856 | tf_op jit(solution)/shard_map/pallas_call | solution.py:496
  27.5 0.0 collective-permute-done.even_far
  27.5 1.0 %collective-permute-done.1.odd_far = f32[3,3,4,128]{3,2,1,0:T(4,128)} collective-permute-done((f32[3,3,4,128]{3,2,1,0:T(4,128)}, f32[3,3,4,128]{3,2,1,0:T(4,128)}, u32[]{:S(2)}, u32[]{:S(2)}) %collective-permute-start.1) | collective-permute-done | bytes 18464 | tf_op jit(solution)/shard_map/ppermute | solution.py:554
  28.4 2.1 %all-to-all-done = f32[256,1,256]{2,1,0:T(1,128)} async-done(((f32[256,1,256]{2,1,0:T(1,128)}), f32[256,1,256]{2,1,0:T(1,128)}, u32[]{:S(2)}, u32[]{:S(2)}) %all-to-all-start) | async-done | bytes 262176 | tf_op jit(solution)/shard_map/all_to_all | solution.py:526
  30.5 4.2 %shard_map.138 = f32[768,128]{1,0:T(8,128)} custom-call(f32[512,128]{1,0:T(8,128)} %bitcast.2.source_far, bf16[2,640,256]{2,1,0:T(8,128)(2,1)} %constant.20.clone.mixing_far, f32[3,256,128]{2,1,0:T(8,128)} %constant.21.clone.turning_far, bf16[2,2,2,128,256]{4,3,2,1,0:T(8,128)(2,1)} %constant.22.clone.lane_backward_far, ...), custom_call_target="tpu_custom_call" | custom-call | flops 1006632960 | bytes 3932160 | tf_op jit(solution)/shard_map/pallas_call | solution.py:496
  34.7 12.2 %all-to-all-start.1 = ((f32[256,1,384]{2,1,0:T(1,128)}), f32[256,1,384]{2,1,0:T(1,128)}, u32[]{:S(2)}, u32[]{:S(2)}) async-start(f32[256,1,384]{2,1,0:T(1,128)} %bitcast.10), calls=%async_computation.1 | async-start | bytes 786432 | tf_op jit(solution)/shard_map/all_to_all | solution.py:585
  46.9 1.7 %shard_map.139 = (f32[288,128]{1,0:T(8,128)}, f32[216,128]{1,0:T(8,128)}, f32[216,128]{1,0:T(8,128)}) custom-call(f32[192,128]{1,0:T(8,128)} %bitcast.11, f32[3,3,4,128]{3,2,1,0:T(4,128)} %collective-permute-done.even_far, f32[3,3,4,128]{3,2,1,0:T(4,128)} %collective-permute-done.1.odd_far), custom_call_target="tpu_custom_call" | custom-call | flops 16777216 | bytes 503808 | tf_op jit(solution)/shard_map/pallas_call | solution.py:496
  48.6 0.2 collective-permute-start.2
  48.8 6.2 %collective-permute-start.3 = (f32[216,128]{1,0:T(8,128)}, f32[216,128]{1,0:T(8,128)}, u32[]{:S(2)}, u32[]{:S(2)}) collective-permute-start(f32[216,128]{1,0:T(8,128)} %get-tuple-element.45), channel_id=1, source_target_pairs={{0,31},{1,2},{2,1},{3,4},{4,3},{5,6},{6,5},{7,8},{8,7},{9,10},{10,... | collective-permute-start | bytes 331784 | tf_op jit(solution)/shard_map/ppermute | solution.py:588
  55.0 0.0 collective-permute-done.2.even
  55.0 6.6 %collective-permute-done.3.odd = f32[216,128]{1,0:T(8,128)} collective-permute-done((f32[216,128]{1,0:T(8,128)}, f32[216,128]{1,0:T(8,128)}, u32[]{:S(2)}, u32[]{:S(2)}) %collective-permute-start.3) | collective-permute-done | bytes 110624 | tf_op jit(solution)/shard_map/ppermute | solution.py:588
  61.6 3.0 %shard_map.140 = (f32[720,128]{1,0:T(8,128)}, f32[1728,256]{1,0:T(8,128)}, f32[576,128]{1,0:T(8,128)}) custom-call(f32[288,128]{1,0:T(8,128)} %get-tuple-element.43.own, f32[216,128]{1,0:T(8,128)} %collective-permute-done.2.even, f32[216,128]{1,0:T(8,128)} %collective-permute-done.3.odd, f32[192,128]{1,0:T(8,128)} %get-tuple-element.46.bias_far, ...), custom_call_target="tpu_custom_call" | custom-call | flops 226492416 | bytes 3084288 | tf_op jit(solution)/shard_map/pallas_call | solution.py:496
  64.6 0.0 all-to-all-done.1
  64.6 4.0 %shard_map.141 = f32[192,128]{1,0:T(8,128)} custom-call(f32[768,128]{1,0:T(8,128)} %bitcast.7.modes_far, bf16[2,2,128,128]{3,2,1,0:T(8,128)(2,1)} %constant.19.clone.table_far, f32[720,128]{1,0:T(8,128)} %get-tuple-element.48.field_far, f32[576,128]{1,0:T(8,128)} %get-tuple-element.49.slants_far, f32[1728,256]{1,0:T(8,128)} %get-tuple-element.50.slope_far, ...), custom_call_target="tpu_custom_call" | custom-call | flops 536870912 | bytes 3629056 | tf_op jit(solution)/shard_map/pallas_call | solution.py:496
Async XLA Ops:
  1.9 28.6 %all-to-all-start = ((f32[256,1,256]{2,1,0:T(1,128)}), f32[256,1,256]{2,1,0:T(1,128)}, u32[]{:S(2)}, u32[]{:S(2)}) async-start(f32[256,1,256]{2,1,0:T(1,128)} %bitcast.12), calls=%async_computation | async-start | bytes 524288 | tf_op jit(solution)/shard_map/all_to_all | solution.py:526
  17.4 10.1 %collective-permute-start = (f32[3,3,4,128]{3,2,1,0:T(4,128)}, f32[3,3,4,128]{3,2,1,0:T(4,128)}, u32[]{:S(2)}, u32[]{:S(2)}) collective-permute-start(f32[3,3,4,128]{3,2,1,0:T(4,128)} %get-tuple-element.31), channel_id=1, source_target_pairs={{0,32},{32,0},{64,96},{96,64},{128,160},{160,128},{192,224},{224,1... | collective-permute-start | bytes 55304 | tf_op jit(solution)/shard_map/ppermute | solution.py:553
  18.3 10.1 %collective-permute-start.1 = (f32[3,3,4,128]{3,2,1,0:T(4,128)}, f32[3,3,4,128]{3,2,1,0:T(4,128)}, u32[]{:S(2)}, u32[]{:S(2)}) collective-permute-start(f32[3,3,4,128]{3,2,1,0:T(4,128)} %get-tuple-element.32), channel_id=1, source_target_pairs={{0,224},{32,64},{64,32},{96,128},{128,96},{160,192},{192,160},{224... | collective-permute-start | bytes 55304 | tf_op jit(solution)/shard_map/ppermute | solution.py:554
  34.7 30.0 %all-to-all-start.1 = ((f32[256,1,384]{2,1,0:T(1,128)}), f32[256,1,384]{2,1,0:T(1,128)}, u32[]{:S(2)}, u32[]{:S(2)}) async-start(f32[256,1,384]{2,1,0:T(1,128)} %bitcast.10), calls=%async_computation.1 | async-start | bytes 786432 | tf_op jit(solution)/shard_map/all_to_all | solution.py:585
  48.6 6.4 %collective-permute-start.2 = (f32[216,128]{1,0:T(8,128)}, f32[216,128]{1,0:T(8,128)}, u32[]{:S(2)}, u32[]{:S(2)}) collective-permute-start(f32[216,128]{1,0:T(8,128)} %get-tuple-element.44), channel_id=1, source_target_pairs={{0,1},{1,0},{2,3},{3,2},{4,5},{5,4},{6,7},{7,6},{8,9},{9,8},{10,11... | collective-permute-start | bytes 331784 | tf_op jit(solution)/shard_map/ppermute | solution.py:587
  48.8 12.8 %collective-permute-start.3 = (f32[216,128]{1,0:T(8,128)}, f32[216,128]{1,0:T(8,128)}, u32[]{:S(2)}, u32[]{:S(2)}) collective-permute-start(f32[216,128]{1,0:T(8,128)} %get-tuple-element.45), channel_id=1, source_target_pairs={{0,31},{1,2},{2,1},{3,4},{4,3},{5,6},{6,5},{7,8},{8,7},{9,10},{10,... | collective-permute-start | bytes 331784 | tf_op jit(solution)/shard_map/ppermute | solution.py:588
